TPU v7x, 32 devices: a whole 2x2x4 slice. The times are simulated.
32 devices in a mesh: wide: 4 (over y, x), narrow: 8 (over z, core).
Axes of the slice: x: 2, y: 2, z: 4, core: 2. Of those that a mesh axis runs over, the one named last changes fastest.
Arguments:
- model: float32 [64, 2, 256, 256], P(('wide', 'narrow')), may hold values from -6 to 6
- observed: float32 [64, 2, 256, 256], P(('wide', 'narrow')), may hold values from -6 to 6
- own_weights: float32 [5, 64, 2, 256, 256], P(None, ('wide', 'narrow')), may hold values from -0.1875 to 0.1875
- partner_weights: float32 [5, 64, 2, 256, 256], P(None, ('wide', 'narrow')), may hold values from -0.1875 to 0.1875
Outputs:
- residual: float32 [64, 2, 256, 256], P(('wide', 'narrow'))
- gradient: float32 [64, 2, 256, 256], P(('wide', 'narrow'))
All inputs are finite; a program needn't handle non-finite values.
Results may differ from a plain program's by a relative error of at most 0.0001.
Values sent between devices are 32-bit elements; how exact they have to be, the bound alone decides.
No kernel may reach another device: no remote copies, remote signals or barrier semaphores. Data moves between devices by JAX's collectives and lax.ppermute only.
A program may use at most 128 MiB of HBM per device.

v0:
```python
import functools
from typing import NamedTuple

import jax
import jax.numpy as jnp
from jax import lax
from jax.experimental import pallas as pl
from jax.experimental.pallas import tpu as pltpu
from jax.sharding import PartitionSpec as P


LEVELS = 5
BF, F32 = jnp.bfloat16, jnp.float32
SHARES = (2, 3, 3, 3, 3, 2)
ORDER = (((9, 0),), ((0, 0),), ((9, 1),), ((1, 0),), ((9, 2),), ((0, 1),), ((0, 3),), ((0, 2),), ((1, 1),), ((0, 4),), ((1, 2),), ((0, 5),), ((2, 0),), ((9, 3),), ((3, 0),), ((9, 4),), ((2, 1),), ((1, 3),), ((4, 0),), ((2, 2),), ((3, 1),), ((1, 4),), ((3, 2),), ((2, 3),), ((4, 1),), ((5, 0),), ((4, 2),), ((1, 5),), ((2, 4), (5, 1)), ((6, 0),), ((3, 3),), ((5, 2),), ((2, 5),), ((3, 4),), ((6, 1),), ((4, 3),), ((6, 2),), ((4, 4),), ((5, 3),), ((3, 5),), ((5, 4),), ((6, 3),), ((4, 5),), ((7, 0),), ((6, 4),), ((7, 2),), ((7, 1),), ((5, 5),), ((8, 0),), ((8, 1),), ((8, 2),), ((6, 5),), ((7, 3),), ((7, 4),), ((8, 3), (8, 4)), ((7, 5),), ((8, 5),))
VMEM = pl.BlockSpec(memory_space=pltpu.VMEM)
HBM = pl.BlockSpec(memory_space=pltpu.HBM)
ANY = pl.BlockSpec(memory_space=pl.ANY)


def split(x):
    high = x.astype(BF)
    return high, (x - high.astype(F32)).astype(BF)


def dot(a, b, transposed):
    return lax.dot_general(a, b, (((1,), (1 if transposed else 0,)), ((), ())), preferred_element_type=F32)


def product(ur, ui, high, low, adjoint):
    rows = ur.shape[0]
    rh, rl = split(ur)
    ih, il = split(ui)
    both = jnp.concatenate([rh, rl, ih, il], 0)
    tops = jnp.concatenate([rh, ih], 0)

    def real(k):
        a, c = dot(both, high[k], adjoint), dot(tops, low[k], adjoint)
        return a[:rows] + a[rows : 2 * rows] + c[:rows], a[2 * rows : 3 * rows] + a[3 * rows :] + c[rows:]

    rr, ir = real(0)
    ri, ii = real(1)
    return (rr + ii, ir - ri) if adjoint else (rr - ii, ri + ir)


def prepare_kernel(level, own, partner, *refs):
    high, low, buffer, sems = refs[-4:]
    boxes = high.shape[1]
    copies = [
        [pltpu.make_async_copy(source.at[level, b], buffer.at[s, b], sems.at[s, b]) for b in range(boxes)]
        for s, source in enumerate((own, partner))
    ]
    for row in copies:
        for copy in row:
            copy.start()
    for s, row in enumerate(copies):
        for b, copy in enumerate(row):
            copy.wait()
            high[s, b], low[s, b] = split(buffer[s, b])


class Task(NamedTuple):
    stage: int
    rows: int
    ours: tuple
    theirs: tuple
    weights: int
    sent: tuple = ()
    kept: int = -1
    observed: int = -1
    result: tuple = ()


def group_kernel(tasks, *refs):
    copies = []
    for task in tasks:
        (ours, start), (theirs, other) = ((refs[ref], pl.ds(row, task.rows)) for ref, row in (task.ours, task.theirs))
        high, low = refs[task.weights], refs[task.weights + 1]
        boxes = range(ours.shape[0])
        if task.sent:
            out, at = refs[task.sent[0]], pl.ds(task.sent[1], task.rows)
        if task.result:
            whole, row, buffer, sems = task.result
            buffer, final = refs[buffer], pl.ds(row, task.rows)
            writes = [
                pltpu.make_async_copy(buffer.at[b], refs[whole].at[b, :, final], refs[sems].at[b]) for b in boxes
            ]
            copies += writes
        if task.stage < LEVELS:
            for b in boxes:
                p = b ^ 1 if task.stage == 0 else b
                r0, i0 = product(ours[b, 0, start], ours[b, 1, start], high.at[0, b], low.at[0, b], False)
                r1, i1 = product(theirs[p, 0, other], theirs[p, 1, other], high.at[1, b], low.at[1, b], False)
                if task.stage < LEVELS - 1:
                    out[b, 0, at], out[b, 1, at] = r0 + r1, i0 + i1
                else:
                    observed = refs[task.observed]
                    buffer[b, 0] = r0 + r1 - observed[b, 0, final]
                    buffer[b, 1] = i0 + i1 - observed[b, 1, final]
                    writes[b].start()
            if task.stage < LEVELS - 1:
                continue
            grads = [(buffer[b, 0], buffer[b, 1]) for b in boxes]
        else:
            grads = [
                (ours[b, 0, start] + theirs[b, 0, other], ours[b, 1, start] + theirs[b, 1, other]) for b in boxes
            ]
        for b in boxes:
            if task.sent:
                out[b, 0, at], out[b, 1, at] = product(*grads[b], high.at[1, b], low.at[1, b], True)
            sr, si = product(*grads[b], high.at[0, b], low.at[0, b], True)
            if task.sent:
                kept = refs[task.kept]
                kept[b, 0], kept[b, 1] = sr, si
            else:
                p = b ^ 1
                tr, ti = product(*grads[p], high.at[1, p], low.at[1, p], True)
                buffer[b, 0], buffer[b, 1] = sr + tr, si + ti
                writes[b].start()
    for copy in copies:
        copy.wait()


def call(kernel, operands, specs, outs, out_specs, scratch=(), aliases=None):
    return pl.pallas_call(
        kernel,
        out_shape=outs,
        in_specs=specs,
        out_specs=out_specs,
        scratch_shapes=scratch,
        input_output_aliases=aliases or {},
        compiler_params=pltpu.CompilerParams(vmem_limit_bytes=10 << 20),
    )(*operands)


def shards(model, observed, own_weights, partner_weights):
    narrow, wide = lax.axis_size("narrow"), lax.axis_size("wide")
    exchanges = {1: ("narrow", 1), 2: ("narrow", narrow // 2), 3: ("wide", 1), 4: ("wide", wide // 2)}
    boxes, parts, rows, k = model.shape
    edges = [sum(SHARES[:c]) * rows // sum(SHARES) for c in range(len(SHARES) + 1)]

    def swap(value, level):
        axis, mask = exchanges[level]
        return lax.ppermute(value, axis, [(i, i ^ mask) for i in range(lax.axis_size(axis))])

    def rows_of(count):
        return pltpu.VMEM((boxes, parts, count, k), F32)

    model, observed = (pltpu.with_memory_space_constraint(x, pltpu.VMEM) for x in (model, observed))
    stored = [pltpu.with_memory_space_constraint(x, pltpu.HBM) for x in (own_weights, partner_weights)]
    matrices = (2,) + own_weights.shape[1:]
    weights = {}
    ours = {c: (model, edges[c]) for c in range(len(SHARES))}
    theirs = dict(ours)
    results = {}
    token = None

    for group in ORDER:
        stage, c = group[0]
        if stage == 9:
            tokens = [] if token is None else [token]
            weights[c] = call(
                functools.partial(prepare_kernel, c),
                stored + tokens,
                [HBM, HBM] + [ANY] * len(tokens),
                (pltpu.VMEM(matrices, BF),) * 2,
                (VMEM, VMEM),
                [pltpu.VMEM(matrices, F32), pltpu.SemaphoreType.DMA((2, boxes))],
            )
            token = weights[c][0]
            continue
        operands, specs, outs, out_specs, scratch, aliases, plans = [], [], [], [], [], {}, []

        def operand(array, spec=VMEM):
            for at, known in enumerate(operands):
                if known is array:
                    return at
            operands.append(array)
            specs.append(spec)
            return len(operands) - 1

        counts = [edges[c + 1] - edges[c] for _, c in group]
        sends = exchange_of(stage)
        if sends:
            outs.append(rows_of(sum(counts)))
            out_specs.append(VMEM)
        else:
            outs.append(pltpu.VMEM((8, 128), F32))
            out_specs.append(VMEM)
        row, places = 0, {}
        for (stage, c), count in zip(group, counts):
            level = level_of(stage)
            plan = {
                "stage": stage,
                "rows": count,
                "ours": (operand(ours[c][0]), ours[c][1]),
                "theirs": (operand(theirs[c][0]), theirs[c][1]),
            }
            pair = [x for x in weights[level]]
            plan["weights"] = next((at for at, known in enumerate(operands) if known is pair[0]), len(operands))
            for x in pair:
                operand(x)
            if sends:
                plan["sent"] = (0, row)
            if LEVELS - 1 <= stage < 8:
                plan["kept"] = len(outs)
                outs.append(rows_of(count))
                out_specs.append(VMEM)
            if stage == LEVELS - 1:
                plan["observed"] = operand(observed)
            if stage in (LEVELS - 1, 8):
                if stage not in places:
                    if stage in results:
                        aliases[operand(results[stage], HBM)] = len(outs)
                    places[stage] = len(outs)
                    outs.append(pltpu.HBM((boxes, parts, rows, k), F32))
                    out_specs.append(HBM)
                plan["result"] = (places[stage], edges[c], len(scratch), len(scratch) + 1)
                scratch += [rows_of(count), pltpu.SemaphoreType.DMA((boxes,))]
            plans.append(plan)
            row += count
        operand(token, ANY)
        first, second = len(operands), len(operands) + len(outs)
        for plan in plans:
            if "sent" in plan:
                plan["sent"] = (first + plan["sent"][0], plan["sent"][1])
            if "kept" in plan:
                plan["kept"] += first
            if "result" in plan:
                whole, at, buffer, sems = plan["result"]
                plan["result"] = (first + whole, at, second + buffer, second + sems)
        tasks = tuple(Task(**plan) for plan in plans)
        made = call(functools.partial(group_kernel, tasks), operands, specs, outs, out_specs, scratch, aliases)
        token = made[0]
        for stage, at in places.items():
            results[stage] = made[at]
        if not sends:
            continue
        received = swap(token, sends)
        for task, (stage, c) in zip(tasks, group):
            at = task.sent[1]
            ours[c] = (token, at) if task.kept < 0 else (made[task.kept - first], 0)
            theirs[c] = (received, at)
    return results[LEVELS - 1], results[8]


def level_of(stage):
    return stage if stage < LEVELS else 2 * LEVELS - 2 - stage


def exchange_of(stage):
    return stage + 1 if stage < LEVELS - 1 else level_of(stage)


def solution(mesh):
    boxes = P(("wide", "narrow"), None, None, None)
    matrices = P(None, ("wide", "narrow"), None, None, None)

    return jax.shard_map(
        shards, mesh=mesh, in_specs=(boxes, boxes, matrices, matrices), out_specs=(boxes, boxes), check_vma=False
    )
```

profile of v0, /device:TPU:1, one launch (start us, length us, event | category | flops | bytes accessed | tf_op | source)
XLA Modules:
  0.0 180.3 jit_solution(15868122052507953867)
XLA Ops:
  0.6 1.7 shard_map.59
  3.0 1.6 shard_map.61
  5.2 1.6 shard_map.63
  9.1 3.8 %collective-permute-start.5 = (f32[2,2,32,256]{3,2,1,0:T(8,128)S(1)}, f32[2,2,32,256]{3,2,1,0:T(8,128)S(1)}, u32[]{:S(2)}, u32[]{:S(2)}) collective-permute-start(f32[2,2,32,256]{3,2,1,0:T(8,128)S(1)} %shard_map.62.refs_0_), channel_id=1, source_target_pairs={{0,4},{1,5},{2,6},{3,7},{4,0},{5,1},{6,2},{7,3},{8,12},{9,13},{10,... | collective-permute-start | bytes 393224 | tf_op jit(solution)/shard_map/ppermute | solution.py:144
  15.1 8.6 %collective-permute-done.5.refs_1_ = f32[2,2,32,256]{3,2,1,0:T(8,128)S(1)} collective-permute-done((f32[2,2,32,256]{3,2,1,0:T(8,128)S(1)}, f32[2,2,32,256]{3,2,1,0:T(8,128)S(1)}, u32[]{:S(2)}, u32[]{:S(2)}) %collective-permute-start.5) | collective-permute-done | bytes 131104 | tf_op jit(solution)/shard_map/ppermute | solution.py:144
  25.2 1.8 collective-permute-start.8
  27.0 1.6 shard_map.72
  29.2 1.6 shard_map.74
  32.1 1.2 collective-permute-start.7
  33.3 2.9 %collective-permute-start.11 = (f32[2,2,48,256]{3,2,1,0:T(8,128)S(1)}, f32[2,2,48,256]{3,2,1,0:T(8,128)S(1)}, u32[]{:S(2)}, u32[]{:S(2)}) collective-permute-start(f32[2,2,48,256]{3,2,1,0:T(8,128)S(1)} %shard_map.68.refs_4_.refs_0_), channel_id=1, source_target_pairs={{0,1},{1,0},{2,3},{3,2},{4,5},{5,4},{6,7},{7,6},{8,9},{9,8},{10,11... | collective-permute-start | bytes 589832 | tf_op jit(solution)/shard_map/ppermute | solution.py:144
  36.8 1.2 shard_map.77
  38.0 2.3 %collective-permute-done.4.refs_1_ = f32[2,2,48,256]{3,2,1,0:T(8,128)S(1)} collective-permute-done((f32[2,2,48,256]{3,2,1,0:T(8,128)S(1)}, f32[2,2,48,256]{3,2,1,0:T(8,128)S(1)}, u32[]{:S(2)}, u32[]{:S(2)}) %collective-permute-start.4) | collective-permute-done | bytes 196640 | tf_op jit(solution)/shard_map/ppermute | solution.py:144
  42.2 1.3 collective-permute-start.14
  44.0 2.5 %collective-permute-done.10.refs_1_ = f32[2,2,48,256]{3,2,1,0:T(8,128)S(1)} collective-permute-done((f32[2,2,48,256]{3,2,1,0:T(8,128)S(1)}, f32[2,2,48,256]{3,2,1,0:T(8,128)S(1)}, u32[]{:S(2)}, u32[]{:S(2)}) %collective-permute-start.10) | collective-permute-done | bytes 196640 | tf_op jit(solution)/shard_map/ppermute | solution.py:144
  47.0 1.3 collective-permute-start.13
  48.3 5.7 %collective-permute-done.15.refs_1_ = f32[2,2,48,256]{3,2,1,0:T(8,128)S(1)} collective-permute-done((f32[2,2,48,256]{3,2,1,0:T(8,128)S(1)}, f32[2,2,48,256]{3,2,1,0:T(8,128)S(1)}, u32[]{:S(2)}, u32[]{:S(2)}) %collective-permute-start.15) | collective-permute-done | bytes 196640 | tf_op jit(solution)/shard_map/ppermute | solution.py:144
  54.6 1.3 shard_map.83
  55.9 3.8 %collective-permute-start.22 = (f32[2,2,48,256]{3,2,1,0:T(8,128)S(1)}, f32[2,2,48,256]{3,2,1,0:T(8,128)S(1)}, u32[]{:S(2)}, u32[]{:S(2)}) collective-permute-start(f32[2,2,48,256]{3,2,1,0:T(8,128)S(1)} %get-tuple-element.89.refs_4_), channel_id=1, source_target_pairs={{0,16},{8,24},{16,0},{24,8},{1,17},{9,25},{17,1},{25,9},{2,18},{10... | collective-permute-start | bytes 589832 | tf_op jit(solution)/shard_map/ppermute | solution.py:144
  59.7 3.0 %collective-permute-start.3 = (f32[2,2,32,256]{3,2,1,0:T(8,128)S(1)}, f32[2,2,32,256]{3,2,1,0:T(8,128)S(1)}, u32[]{:S(2)}, u32[]{:S(2)}) collective-permute-start(f32[2,2,32,256]{3,2,1,0:T(8,128)S(1)} %shard_map.70.refs_4_.refs_0_), channel_id=1, source_target_pairs={{0,1},{1,0},{2,3},{3,2},{4,5},{5,4},{6,7},{7,6},{8,9},{9,8},{10,11... | collective-permute-start | bytes 393224 | tf_op jit(solution)/shard_map/ppermute | solution.py:144
  62.7 2.3 %collective-permute-done.16.refs_1_ = f32[2,2,32,256]{3,2,1,0:T(8,128)S(1)} collective-permute-done((f32[2,2,32,256]{3,2,1,0:T(8,128)S(1)}, f32[2,2,32,256]{3,2,1,0:T(8,128)S(1)}, u32[]{:S(2)}, u32[]{:S(2)}) %collective-permute-start.16) | collective-permute-done | bytes 131104 | tf_op jit(solution)/shard_map/ppermute | solution.py:144
  65.7 1.5 shard_map.85
  67.7 1.2 shard_map.87
  68.9 4.1 %collective-permute-start.25 = (f32[2,2,96,256]{3,2,1,0:T(8,128)S(1)}, f32[2,2,96,256]{3,2,1,0:T(8,128)S(1)}, u32[]{:S(2)}, u32[]{:S(2)}) collective-permute-start(f32[2,2,96,256]{3,2,1,0:T(8,128)S(1)} %get-tuple-element.95.refs_4_.refs_0_), channel_id=1, source_target_pairs={{0,8},{8,0},{16,24},{24,16},{1,9},{9,1},{17,25},{25,17},{2,10},{10... | collective-permute-start | bytes 1179656 | tf_op jit(solution)/shard_map/ppermute | solution.py:144
  73.1 1.4 collective-permute-start.20
  74.4 1.2 collective-permute-start.18
  75.7 12.4 %collective-permute-done.20.refs_1_ = f32[2,2,32,256]{3,2,1,0:T(8,128)S(1)} collective-permute-done((f32[2,2,32,256]{3,2,1,0:T(8,128)S(1)}, f32[2,2,32,256]{3,2,1,0:T(8,128)S(1)}, u32[]{:S(2)}, u32[]{:S(2)}) %collective-permute-start.20) | collective-permute-done | bytes 131104 | tf_op jit(solution)/shard_map/ppermute | solution.py:144
  89.4 1.3 collective-permute-start.24
  91.5 1.2 collective-permute-start.28
  92.7 2.8 %collective-permute-done.17.refs_1_ = f32[2,2,32,256]{3,2,1,0:T(8,128)S(1)} collective-permute-done((f32[2,2,32,256]{3,2,1,0:T(8,128)S(1)}, f32[2,2,32,256]{3,2,1,0:T(8,128)S(1)}, u32[]{:S(2)}, u32[]{:S(2)}) %collective-permute-start.17) | collective-permute-done | bytes 131104 | tf_op jit(solution)/shard_map/ppermute | solution.py:144
  97.6 1.3 shard_map.94
  98.9 1.3 collective-permute-start.26
  101.1 1.3 shard_map.96
  102.7 1.6 collective-permute-done.26.refs_1_
  106.6 4.5 %collective-permute-done.23.refs_1_ = f32[2,2,32,256]{3,2,1,0:T(8,128)S(1)} collective-permute-done((f32[2,2,32,256]{3,2,1,0:T(8,128)S(1)}, f32[2,2,32,256]{3,2,1,0:T(8,128)S(1)}, u32[]{:S(2)}, u32[]{:S(2)}) %collective-permute-start.23) | collective-permute-done | bytes 131104 | tf_op jit(solution)/shard_map/ppermute | solution.py:144
  111.6 2.6 %collective-permute-start.29 = (f32[2,2,32,256]{3,2,1,0:T(8,128)S(1)}, f32[2,2,32,256]{3,2,1,0:T(8,128)S(1)}, u32[]{:S(2)}, u32[]{:S(2)}) collective-permute-start(f32[2,2,32,256]{3,2,1,0:T(8,128)S(1)} %shard_map.98.refs_4_.refs_0_), channel_id=1, source_target_pairs={{0,16},{8,24},{16,0},{24,8},{1,17},{9,25},{17,1},{25,9},{2,18},{10... | collective-permute-start | bytes 393224 | tf_op jit(solution)/shard_map/ppermute | solution.py:144
  116.3 2.1 %collective-permute-start.33 = (f32[2,2,48,256]{3,2,1,0:T(8,128)S(1)}, f32[2,2,48,256]{3,2,1,0:T(8,128)S(1)}, u32[]{:S(2)}, u32[]{:S(2)}) collective-permute-start(f32[2,2,48,256]{3,2,1,0:T(8,128)S(1)} %get-tuple-element.100.refs_6_), channel_id=1, source_target_pairs={{0,4},{1,5},{2,6},{3,7},{4,0},{5,1},{6,2},{7,3},{8,12},{9,13},{10,... | collective-permute-start | bytes 589832 | tf_op jit(solution)/shard_map/ppermute | solution.py:144
  119.4 1.2 shard_map.101
  120.7 19.8 %collective-permute-done.36.refs_1_ = f32[2,2,32,256]{3,2,1,0:T(8,128)S(1)} collective-permute-done((f32[2,2,32,256]{3,2,1,0:T(8,128)S(1)}, f32[2,2,32,256]{3,2,1,0:T(8,128)S(1)}, u32[]{:S(2)}, u32[]{:S(2)}) %collective-permute-start.36) | collective-permute-done | bytes 131104 | tf_op jit(solution)/shard_map/ppermute | solution.py:144
  141.3 2.0 %collective-permute-start.40 = (f32[2,2,32,256]{3,2,1,0:T(8,128)S(1)}, f32[2,2,32,256]{3,2,1,0:T(8,128)S(1)}, u32[]{:S(2)}, u32[]{:S(2)}) collective-permute-start(f32[2,2,32,256]{3,2,1,0:T(8,128)S(1)} %get-tuple-element.120.refs_4_), channel_id=1, source_target_pairs={{0,1},{1,0},{2,3},{3,2},{4,5},{5,4},{6,7},{7,6},{8,9},{9,8},{10,11... | collective-permute-start | bytes 393224 | tf_op jit(solution)/shard_map/ppermute | solution.py:144
  146.3 2.4 %collective-permute-start.44 = (f32[2,2,48,256]{3,2,1,0:T(8,128)S(1)}, f32[2,2,48,256]{3,2,1,0:T(8,128)S(1)}, u32[]{:S(2)}, u32[]{:S(2)}) collective-permute-start(f32[2,2,48,256]{3,2,1,0:T(8,128)S(1)} %get-tuple-element.121.refs_4_), channel_id=1, source_target_pairs={{0,4},{1,5},{2,6},{3,7},{4,0},{5,1},{6,2},{7,3},{8,12},{9,13},{10,... | collective-permute-start | bytes 589832 | tf_op jit(solution)/shard_map/ppermute | solution.py:144
  149.9 1.4 shard_map.107
  151.4 1.5 shard_map.108
  152.9 1.7 shard_map.109
  155.4 5.9 %collective-permute-done.42.refs_1_ = f32[2,2,48,256]{3,2,1,0:T(8,128)S(1)} collective-permute-done((f32[2,2,48,256]{3,2,1,0:T(8,128)S(1)}, f32[2,2,48,256]{3,2,1,0:T(8,128)S(1)}, u32[]{:S(2)}, u32[]{:S(2)}) %collective-permute-start.42) | collective-permute-done | bytes 196640 | tf_op jit(solution)/shard_map/ppermute | solution.py:144
  162.1 3.4 %collective-permute-done.44.refs_1_ = f32[2,2,48,256]{3,2,1,0:T(8,128)S(1)} collective-permute-done((f32[2,2,48,256]{3,2,1,0:T(8,128)S(1)}, f32[2,2,48,256]{3,2,1,0:T(8,128)S(1)}, u32[]{:S(2)}, u32[]{:S(2)}) %collective-permute-start.44) | collective-permute-done | bytes 196640 | tf_op jit(solution)/shard_map/ppermute | solution.py:144
  168.2 2.2 %shard_map.113 = (f32[8,128]{1,0:T(8,128)S(1)}, f32[2,2,256,256]{3,2,1,0:T(8,128)}) custom-call(f32[2,2,48,256]{3,2,1,0:T(8,128)S(1)} %get-tuple-element.137.refs_0_, f32[2,2,48,256]{3,2,1,0:T(8,128)S(1)} %collective-permute-done.43.refs_1_, bf16[2,2,2,256,256]{4,3,2,1,0:T(8,128)(2,1)S(1)} %get-tuple-element.75.refs_1_.refs_2_, ...), custom_call_target="tpu_custom_call", output_to_operand_aliasing={{1}: (4, {})} | custom-call | tf_op jit(solution)/shard_map/pallas_call | solution.py:125
  170.4 5.4 %collective-permute-done.41.refs_1_ = f32[2,2,32,256]{3,2,1,0:T(8,128)S(1)} collective-permute-done((f32[2,2,32,256]{3,2,1,0:T(8,128)S(1)}, f32[2,2,32,256]{3,2,1,0:T(8,128)S(1)}, u32[]{:S(2)}, u32[]{:S(2)}) %collective-permute-start.41) | collective-permute-done | bytes 131104 | tf_op jit(solution)/shard_map/ppermute | solution.py:144
  178.0 2.0 %shard_map.115 = (f32[8,128]{1,0:T(8,128)}, f32[2,2,256,256]{3,2,1,0:T(8,128)}) custom-call(f32[2,2,32,256]{3,2,1,0:T(8,128)S(1)} %get-tuple-element.144.refs_0_, f32[2,2,32,256]{3,2,1,0:T(8,128)S(1)} %collective-permute-done.46.refs_1_, bf16[2,2,2,256,256]{4,3,2,1,0:T(8,128)(2,1)S(1)} %get-tuple-element.75.refs_1_.refs_2_, ...), custom_call_target="tpu_custom_call", output_to_operand_aliasing={{1}: (4, {})} | custom-call | tf_op jit(solution)/shard_map/pallas_call | solution.py:125
  (107 shorter events, 37.3 us)
Async XLA Ops:
  3.0 1.7 collective-permute-start
  7.4 5.5 %collective-permute-start.2 = (f32[2,2,48,256]{3,2,1,0:T(8,128)S(1)}, f32[2,2,48,256]{3,2,1,0:T(8,128)S(1)}, u32[]{:S(2)}, u32[]{:S(2)}) collective-permute-start(f32[2,2,48,256]{3,2,1,0:T(8,128)S(1)} %shard_map.64.refs_3_.refs_0_), channel_id=1, source_target_pairs={{0,1},{1,0},{2,3},{3,2},{4,5},{5,4},{6,7},{7,6},{8,9},{9,8},{10,11... | collective-permute-start | bytes 589832 | tf_op jit(solution)/shard_map/ppermute | solution.py:144
  9.0 5.0 %collective-permute-start.1 = (f32[2,2,48,256]{3,2,1,0:T(8,128)S(1)}, f32[2,2,48,256]{3,2,1,0:T(8,128)S(1)}, u32[]{:S(2)}, u32[]{:S(2)}) collective-permute-start(f32[2,2,48,256]{3,2,1,0:T(8,128)S(1)} %shard_map.66.refs_4_.refs_0_), channel_id=1, source_target_pairs={{0,1},{1,0},{2,3},{3,2},{4,5},{5,4},{6,7},{7,6},{8,9},{9,8},{10,11... | collective-permute-start | bytes 589832 | tf_op jit(solution)/shard_map/ppermute | solution.py:144
  9.1 14.6 %collective-permute-start.5 = (f32[2,2,32,256]{3,2,1,0:T(8,128)S(1)}, f32[2,2,32,256]{3,2,1,0:T(8,128)S(1)}, u32[]{:S(2)}, u32[]{:S(2)}) collective-permute-start(f32[2,2,32,256]{3,2,1,0:T(8,128)S(1)} %shard_map.62.refs_0_), channel_id=1, source_target_pairs={{0,4},{1,5},{2,6},{3,7},{4,0},{5,1},{6,2},{7,3},{8,12},{9,13},{10,... | collective-permute-start | bytes 393224 | tf_op jit(solution)/shard_map/ppermute | solution.py:144
  13.4 17.4 %collective-permute-start.9 = (f32[2,2,48,256]{3,2,1,0:T(8,128)S(1)}, f32[2,2,48,256]{3,2,1,0:T(8,128)S(1)}, u32[]{:S(2)}, u32[]{:S(2)}) collective-permute-start(f32[2,2,48,256]{3,2,1,0:T(8,128)S(1)} %shard_map.67.refs_3_.refs_0_), channel_id=1, source_target_pairs={{0,4},{1,5},{2,6},{3,7},{4,0},{5,1},{6,2},{7,3},{8,12},{9,13},{10,... | collective-permute-start | bytes 589832 | tf_op jit(solution)/shard_map/ppermute | solution.py:144
  24.2 4.5 %collective-permute-start.6 = (f32[2,2,32,256]{3,2,1,0:T(8,128)S(1)}, f32[2,2,32,256]{3,2,1,0:T(8,128)S(1)}, u32[]{:S(2)}, u32[]{:S(2)}) collective-permute-start(f32[2,2,32,256]{3,2,1,0:T(8,128)S(1)} %shard_map.71.refs_0_), channel_id=1, source_target_pairs={{0,8},{8,0},{16,24},{24,16},{1,9},{9,1},{17,25},{25,17},{2,10},{10... | collective-permute-start | bytes 393224 | tf_op jit(solution)/shard_map/ppermute | solution.py:144
  25.2 11.0 %collective-permute-start.8 = (f32[2,2,48,256]{3,2,1,0:T(8,128)S(1)}, f32[2,2,48,256]{3,2,1,0:T(8,128)S(1)}, u32[]{:S(2)}, u32[]{:S(2)}) collective-permute-start(f32[2,2,48,256]{3,2,1,0:T(8,128)S(1)} %shard_map.65.refs_3_.refs_0_), channel_id=1, source_target_pairs={{0,1},{1,0},{2,3},{3,2},{4,5},{5,4},{6,7},{7,6},{8,9},{9,8},{10,11... | collective-permute-start | bytes 589832 | tf_op jit(solution)/shard_map/ppermute | solution.py:144
  28.6 11.6 %collective-permute-start.4 = (f32[2,2,48,256]{3,2,1,0:T(8,128)S(1)}, f32[2,2,48,256]{3,2,1,0:T(8,128)S(1)}, u32[]{:S(2)}, u32[]{:S(2)}) collective-permute-start(f32[2,2,48,256]{3,2,1,0:T(8,128)S(1)} %shard_map.69.refs_3_.refs_0_), channel_id=1, source_target_pairs={{0,4},{1,5},{2,6},{3,7},{4,0},{5,1},{6,2},{7,3},{8,12},{9,13},{10,... | collective-permute-start | bytes 589832 | tf_op jit(solution)/shard_map/ppermute | solution.py:144
  30.9 5.9 %copy-start.1 = (f32[2,2,256,256]{3,2,1,0:T(8,128)S(1)}, f32[2,2,256,256]{3,2,1,0:T(8,128)}, u32[]{:S(2)}) copy-start(f32[2,2,256,256]{3,2,1,0:T(8,128)} %refs_4_.11) | copy-start | bytes 3145732
  31.4 10.2 %collective-permute-start.12 = (f32[2,2,48,256]{3,2,1,0:T(8,128)S(1)}, f32[2,2,48,256]{3,2,1,0:T(8,128)S(1)}, u32[]{:S(2)}, u32[]{:S(2)}) collective-permute-start(f32[2,2,48,256]{3,2,1,0:T(8,128)S(1)} %shard_map.75.refs_4_.refs_0_), channel_id=1, source_target_pairs={{0,8},{8,0},{16,24},{24,16},{1,9},{9,1},{17,25},{25,17},{2,10},{10... | collective-permute-start | bytes 589832 | tf_op jit(solution)/shard_map/ppermute | solution.py:144
  32.1 4.7 %collective-permute-start.7 = (f32[2,2,32,256]{3,2,1,0:T(8,128)S(1)}, f32[2,2,32,256]{3,2,1,0:T(8,128)S(1)}, u32[]{:S(2)}, u32[]{:S(2)}) collective-permute-start(f32[2,2,32,256]{3,2,1,0:T(8,128)S(1)} %shard_map.73.refs_0_), channel_id=1, source_target_pairs={{0,16},{8,24},{16,0},{24,8},{1,17},{9,25},{17,1},{25,9},{2,18},{10... | collective-permute-start | bytes 393224 | tf_op jit(solution)/shard_map/ppermute | solution.py:144
  33.3 10.1 %collective-permute-start.11 = (f32[2,2,48,256]{3,2,1,0:T(8,128)S(1)}, f32[2,2,48,256]{3,2,1,0:T(8,128)S(1)}, u32[]{:S(2)}, u32[]{:S(2)}) collective-permute-start(f32[2,2,48,256]{3,2,1,0:T(8,128)S(1)} %shard_map.68.refs_4_.refs_0_), channel_id=1, source_target_pairs={{0,1},{1,0},{2,3},{3,2},{4,5},{5,4},{6,7},{7,6},{8,9},{9,8},{10,11... | collective-permute-start | bytes 589832 | tf_op jit(solution)/shard_map/ppermute | solution.py:144
  40.8 5.7 %collective-permute-start.10 = (f32[2,2,48,256]{3,2,1,0:T(8,128)S(1)}, f32[2,2,48,256]{3,2,1,0:T(8,128)S(1)}, u32[]{:S(2)}, u32[]{:S(2)}) collective-permute-start(f32[2,2,48,256]{3,2,1,0:T(8,128)S(1)} %shard_map.78.refs_4_.refs_0_), channel_id=1, source_target_pairs={{0,8},{8,0},{16,24},{24,16},{1,9},{9,1},{17,25},{25,17},{2,10},{10... | collective-permute-start | bytes 589832 | tf_op jit(solution)/shard_map/ppermute | solution.py:144
  40.9 13.1 %collective-permute-start.15 = (f32[2,2,48,256]{3,2,1,0:T(8,128)S(1)}, f32[2,2,48,256]{3,2,1,0:T(8,128)S(1)}, u32[]{:S(2)}, u32[]{:S(2)}) collective-permute-start(f32[2,2,48,256]{3,2,1,0:T(8,128)S(1)} %shard_map.76.refs_5_.refs_0_), channel_id=1, source_target_pairs={{0,4},{1,5},{2,6},{3,7},{4,0},{5,1},{6,2},{7,3},{8,12},{9,13},{10,... | collective-permute-start | bytes 589832 | tf_op jit(solution)/shard_map/ppermute | solution.py:144
  42.2 12.4 %collective-permute-start.14 = (f32[2,2,48,256]{3,2,1,0:T(8,128)S(1)}, f32[2,2,48,256]{3,2,1,0:T(8,128)S(1)}, u32[]{:S(2)}, u32[]{:S(2)}) collective-permute-start(f32[2,2,48,256]{3,2,1,0:T(8,128)S(1)} %shard_map.79.refs_4_.refs_0_), channel_id=1, source_target_pairs={{0,16},{8,24},{16,0},{24,8},{1,17},{9,25},{17,1},{25,9},{2,18},{10... | collective-permute-start | bytes 589832 | tf_op jit(solution)/shard_map/ppermute | solution.py:144
  47.0 18.7 %collective-permute-start.13 = (f32[2,2,48,256]{3,2,1,0:T(8,128)S(1)}, f32[2,2,48,256]{3,2,1,0:T(8,128)S(1)}, u32[]{:S(2)}, u32[]{:S(2)}) collective-permute-start(f32[2,2,48,256]{3,2,1,0:T(8,128)S(1)} %shard_map.81.refs_4_.refs_0_), channel_id=1, source_target_pairs={{0,16},{8,24},{16,0},{24,8},{1,17},{9,25},{17,1},{25,9},{2,18},{10... | collective-permute-start | bytes 589832 | tf_op jit(solution)/shard_map/ppermute | solution.py:144
  48.3 19.3 %collective-permute-start.21 = (f32[2,2,48,256]{3,2,1,0:T(8,128)S(1)}, f32[2,2,48,256]{3,2,1,0:T(8,128)S(1)}, u32[]{:S(2)}, u32[]{:S(2)}) collective-permute-start(f32[2,2,48,256]{3,2,1,0:T(8,128)S(1)} %shard_map.80.refs_4_.refs_0_), channel_id=1, source_target_pairs={{0,4},{1,5},{2,6},{3,7},{4,0},{5,1},{6,2},{7,3},{8,12},{9,13},{10,... | collective-permute-start | bytes 589832 | tf_op jit(solution)/shard_map/ppermute | solution.py:144
  55.9 11.8 %collective-permute-start.22 = (f32[2,2,48,256]{3,2,1,0:T(8,128)S(1)}, f32[2,2,48,256]{3,2,1,0:T(8,128)S(1)}, u32[]{:S(2)}, u32[]{:S(2)}) collective-permute-start(f32[2,2,48,256]{3,2,1,0:T(8,128)S(1)} %get-tuple-element.89.refs_4_), channel_id=1, source_target_pairs={{0,16},{8,24},{16,0},{24,8},{1,17},{9,25},{17,1},{25,9},{2,18},{10... | collective-permute-start | bytes 589832 | tf_op jit(solution)/shard_map/ppermute | solution.py:144
  59.6 5.3 %collective-permute-start.16 = (f32[2,2,32,256]{3,2,1,0:T(8,128)S(1)}, f32[2,2,32,256]{3,2,1,0:T(8,128)S(1)}, u32[]{:S(2)}, u32[]{:S(2)}) collective-permute-start(f32[2,2,32,256]{3,2,1,0:T(8,128)S(1)} %get-tuple-element.85.refs_4_), channel_id=1, source_target_pairs={{0,16},{8,24},{16,0},{24,8},{1,17},{9,25},{17,1},{25,9},{2,18},{10... | collective-permute-start | bytes 393224 | tf_op jit(solution)/shard_map/ppermute | solution.py:144
  59.7 7.5 %collective-permute-start.3 = (f32[2,2,32,256]{3,2,1,0:T(8,128)S(1)}, f32[2,2,32,256]{3,2,1,0:T(8,128)S(1)}, u32[]{:S(2)}, u32[]{:S(2)}) collective-permute-start(f32[2,2,32,256]{3,2,1,0:T(8,128)S(1)} %shard_map.70.refs_4_.refs_0_), channel_id=1, source_target_pairs={{0,1},{1,0},{2,3},{3,2},{4,5},{5,4},{6,7},{7,6},{8,9},{9,8},{10,11... | collective-permute-start | bytes 393224 | tf_op jit(solution)/shard_map/ppermute | solution.py:144
  68.9 27.1 %collective-permute-start.25 = (f32[2,2,96,256]{3,2,1,0:T(8,128)S(1)}, f32[2,2,96,256]{3,2,1,0:T(8,128)S(1)}, u32[]{:S(2)}, u32[]{:S(2)}) collective-permute-start(f32[2,2,96,256]{3,2,1,0:T(8,128)S(1)} %get-tuple-element.95.refs_4_.refs_0_), channel_id=1, source_target_pairs={{0,8},{8,0},{16,24},{24,16},{1,9},{9,1},{17,25},{25,17},{2,10},{10... | collective-permute-start | bytes 1179656 | tf_op jit(solution)/shard_map/ppermute | solution.py:144
  73.0 15.8 %collective-permute-start.19 = (f32[2,2,48,256]{3,2,1,0:T(8,128)S(1)}, f32[2,2,48,256]{3,2,1,0:T(8,128)S(1)}, u32[]{:S(2)}, u32[]{:S(2)}) collective-permute-start(f32[2,2,48,256]{3,2,1,0:T(8,128)S(1)} %shard_map.82.refs_6_.refs_0_), channel_id=1, source_target_pairs={{0,8},{8,0},{16,24},{24,16},{1,9},{9,1},{17,25},{25,17},{2,10},{10... | collective-permute-start | bytes 589832 | tf_op jit(solution)/shard_map/ppermute | solution.py:144
  73.1 15.0 %collective-permute-start.20 = (f32[2,2,32,256]{3,2,1,0:T(8,128)S(1)}, f32[2,2,32,256]{3,2,1,0:T(8,128)S(1)}, u32[]{:S(2)}, u32[]{:S(2)}) collective-permute-start(f32[2,2,32,256]{3,2,1,0:T(8,128)S(1)} %get-tuple-element.90.refs_6_), channel_id=1, source_target_pairs={{0,8},{8,0},{16,24},{24,16},{1,9},{9,1},{17,25},{25,17},{2,10},{10... | collective-permute-start | bytes 393224 | tf_op jit(solution)/shard_map/ppermute | solution.py:144
  74.4 16.2 %collective-permute-start.18 = (f32[2,2,48,256]{3,2,1,0:T(8,128)S(1)}, f32[2,2,48,256]{3,2,1,0:T(8,128)S(1)}, u32[]{:S(2)}, u32[]{:S(2)}) collective-permute-start(f32[2,2,48,256]{3,2,1,0:T(8,128)S(1)} %get-tuple-element.91.refs_4_), channel_id=1, source_target_pairs={{0,16},{8,24},{16,0},{24,8},{1,17},{9,25},{17,1},{25,9},{2,18},{10... | collective-permute-start | bytes 589832 | tf_op jit(solution)/shard_map/ppermute | solution.py:144
  89.4 8.3 %collective-permute-start.24 = (f32[2,2,48,256]{3,2,1,0:T(8,128)S(1)}, f32[2,2,48,256]{3,2,1,0:T(8,128)S(1)}, u32[]{:S(2)}, u32[]{:S(2)}) collective-permute-start(f32[2,2,48,256]{3,2,1,0:T(8,128)S(1)} %shard_map.89.refs_4_.refs_0_), channel_id=1, source_target_pairs={{0,16},{8,24},{16,0},{24,8},{1,17},{9,25},{17,1},{25,9},{2,18},{10... | collective-permute-start | bytes 589832 | tf_op jit(solution)/shard_map/ppermute | solution.py:144
  90.7 4.9 %collective-permute-start.17 = (f32[2,2,32,256]{3,2,1,0:T(8,128)S(1)}, f32[2,2,32,256]{3,2,1,0:T(8,128)S(1)}, u32[]{:S(2)}, u32[]{:S(2)}) collective-permute-start(f32[2,2,32,256]{3,2,1,0:T(8,128)S(1)} %shard_map.86.refs_8_.refs_0_), channel_id=1, source_target_pairs={{0,4},{1,5},{2,6},{3,7},{4,0},{5,1},{6,2},{7,3},{8,12},{9,13},{10,... | collective-permute-start | bytes 393224 | tf_op jit(solution)/shard_map/ppermute | solution.py:144
  91.5 8.8 %collective-permute-start.28 = (f32[2,2,48,256]{3,2,1,0:T(8,128)S(1)}, f32[2,2,48,256]{3,2,1,0:T(8,128)S(1)}, u32[]{:S(2)}, u32[]{:S(2)}) collective-permute-start(f32[2,2,48,256]{3,2,1,0:T(8,128)S(1)} %get-tuple-element.97.refs_4_), channel_id=1, source_target_pairs={{0,8},{8,0},{16,24},{24,16},{1,9},{9,1},{17,25},{25,17},{2,10},{10... | collective-permute-start | bytes 589832 | tf_op jit(solution)/shard_map/ppermute | solution.py:144
  96.6 4.6 %collective-permute-start.27 = (f32[2,2,48,256]{3,2,1,0:T(8,128)S(1)}, f32[2,2,48,256]{3,2,1,0:T(8,128)S(1)}, u32[]{:S(2)}, u32[]{:S(2)}) collective-permute-start(f32[2,2,48,256]{3,2,1,0:T(8,128)S(1)} %shard_map.92.refs_4_.refs_0_), channel_id=1, source_target_pairs={{0,16},{8,24},{16,0},{24,8},{1,17},{9,25},{17,1},{25,9},{2,18},{10... | collective-permute-start | bytes 589832 | tf_op jit(solution)/shard_map/ppermute | solution.py:144
  98.9 5.4 %collective-permute-start.26 = (f32[2,2,48,256]{3,2,1,0:T(8,128)S(1)}, f32[2,2,48,256]{3,2,1,0:T(8,128)S(1)}, u32[]{:S(2)}, u32[]{:S(2)}) collective-permute-start(f32[2,2,48,256]{3,2,1,0:T(8,128)S(1)} %get-tuple-element.102.refs_4_), channel_id=1, source_target_pairs={{0,16},{8,24},{16,0},{24,8},{1,17},{9,25},{17,1},{25,9},{2,18},{10... | collective-permute-start | bytes 589832 | tf_op jit(solution)/shard_map/ppermute | solution.py:144
  102.4 11.7 %collective-permute-start.31 = (f32[2,2,48,256]{3,2,1,0:T(8,128)S(1)}, f32[2,2,48,256]{3,2,1,0:T(8,128)S(1)}, u32[]{:S(2)}, u32[]{:S(2)}) collective-permute-start(f32[2,2,48,256]{3,2,1,0:T(8,128)S(1)} %get-tuple-element.106.refs_4_), channel_id=1, source_target_pairs={{0,16},{8,24},{16,0},{24,8},{1,17},{9,25},{17,1},{25,9},{2,18},{10... | collective-permute-start | bytes 589832 | tf_op jit(solution)/shard_map/ppermute | solution.py:144
  105.1 13.3 %collective-permute-start.30 = (f32[2,2,48,256]{3,2,1,0:T(8,128)S(1)}, f32[2,2,48,256]{3,2,1,0:T(8,128)S(1)}, u32[]{:S(2)}, u32[]{:S(2)}) collective-permute-start(f32[2,2,48,256]{3,2,1,0:T(8,128)S(1)} %get-tuple-element.107.refs_4_), channel_id=1, source_target_pairs={{0,8},{8,0},{16,24},{24,16},{1,9},{9,1},{17,25},{25,17},{2,10},{10... | collective-permute-start | bytes 589832 | tf_op jit(solution)/shard_map/ppermute | solution.py:144
  106.2 4.9 %collective-permute-start.23 = (f32[2,2,32,256]{3,2,1,0:T(8,128)S(1)}, f32[2,2,32,256]{3,2,1,0:T(8,128)S(1)}, u32[]{:S(2)}, u32[]{:S(2)}) collective-permute-start(f32[2,2,32,256]{3,2,1,0:T(8,128)S(1)} %shard_map.91.refs_4_.refs_0_), channel_id=1, source_target_pairs={{0,8},{8,0},{16,24},{24,16},{1,9},{9,1},{17,25},{25,17},{2,10},{10... | collective-permute-start | bytes 393224 | tf_op jit(solution)/shard_map/ppermute | solution.py:144
  111.6 7.9 %collective-permute-start.29 = (f32[2,2,32,256]{3,2,1,0:T(8,128)S(1)}, f32[2,2,32,256]{3,2,1,0:T(8,128)S(1)}, u32[]{:S(2)}, u32[]{:S(2)}) collective-permute-start(f32[2,2,32,256]{3,2,1,0:T(8,128)S(1)} %shard_map.98.refs_4_.refs_0_), channel_id=1, source_target_pairs={{0,16},{8,24},{16,0},{24,8},{1,17},{9,25},{17,1},{25,9},{2,18},{10... | collective-permute-start | bytes 393224 | tf_op jit(solution)/shard_map/ppermute | solution.py:144
  114.9 28.4 %collective-permute-start.35 = (f32[2,2,48,256]{3,2,1,0:T(8,128)S(1)}, f32[2,2,48,256]{3,2,1,0:T(8,128)S(1)}, u32[]{:S(2)}, u32[]{:S(2)}) collective-permute-start(f32[2,2,48,256]{3,2,1,0:T(8,128)S(1)} %get-tuple-element.111.refs_4_), channel_id=1, source_target_pairs={{0,8},{8,0},{16,24},{24,16},{1,9},{9,1},{17,25},{25,17},{2,10},{10... | collective-permute-start | bytes 589832 | tf_op jit(solution)/shard_map/ppermute | solution.py:144
  116.0 28.1 %collective-permute-start.34 = (f32[2,2,48,256]{3,2,1,0:T(8,128)S(1)}, f32[2,2,48,256]{3,2,1,0:T(8,128)S(1)}, u32[]{:S(2)}, u32[]{:S(2)}) collective-permute-start(f32[2,2,48,256]{3,2,1,0:T(8,128)S(1)} %get-tuple-element.105.refs_6_), channel_id=1, source_target_pairs={{0,4},{1,5},{2,6},{3,7},{4,0},{5,1},{6,2},{7,3},{8,12},{9,13},{10,... | collective-permute-start | bytes 589832 | tf_op jit(solution)/shard_map/ppermute | solution.py:144
  116.3 28.6 %collective-permute-start.33 = (f32[2,2,48,256]{3,2,1,0:T(8,128)S(1)}, f32[2,2,48,256]{3,2,1,0:T(8,128)S(1)}, u32[]{:S(2)}, u32[]{:S(2)}) collective-permute-start(f32[2,2,48,256]{3,2,1,0:T(8,128)S(1)} %get-tuple-element.100.refs_6_), channel_id=1, source_target_pairs={{0,4},{1,5},{2,6},{3,7},{4,0},{5,1},{6,2},{7,3},{8,12},{9,13},{10,... | collective-permute-start | bytes 589832 | tf_op jit(solution)/shard_map/ppermute | solution.py:144
  118.4 22.2 %collective-permute-start.36 = (f32[2,2,32,256]{3,2,1,0:T(8,128)S(1)}, f32[2,2,32,256]{3,2,1,0:T(8,128)S(1)}, u32[]{:S(2)}, u32[]{:S(2)}) collective-permute-start(f32[2,2,32,256]{3,2,1,0:T(8,128)S(1)} %get-tuple-element.96.refs_4_), channel_id=1, source_target_pairs={{0,4},{1,5},{2,6},{3,7},{4,0},{5,1},{6,2},{7,3},{8,12},{9,13},{10,... | collective-permute-start | bytes 393224 | tf_op jit(solution)/shard_map/ppermute | solution.py:144
  120.7 25.6 %collective-permute-start.32 = (f32[2,2,32,256]{3,2,1,0:T(8,128)S(1)}, f32[2,2,32,256]{3,2,1,0:T(8,128)S(1)}, u32[]{:S(2)}, u32[]{:S(2)}) collective-permute-start(f32[2,2,32,256]{3,2,1,0:T(8,128)S(1)} %get-tuple-element.115.refs_4_), channel_id=1, source_target_pairs={{0,16},{8,24},{16,0},{24,8},{1,17},{9,25},{17,1},{25,9},{2,18},{10... | collective-permute-start | bytes 393224 | tf_op jit(solution)/shard_map/ppermute | solution.py:144
  141.3 8.1 %collective-permute-start.40 = (f32[2,2,32,256]{3,2,1,0:T(8,128)S(1)}, f32[2,2,32,256]{3,2,1,0:T(8,128)S(1)}, u32[]{:S(2)}, u32[]{:S(2)}) collective-permute-start(f32[2,2,32,256]{3,2,1,0:T(8,128)S(1)} %get-tuple-element.120.refs_4_), channel_id=1, source_target_pairs={{0,1},{1,0},{2,3},{3,2},{4,5},{5,4},{6,7},{7,6},{8,9},{9,8},{10,11... | collective-permute-start | bytes 393224 | tf_op jit(solution)/shard_map/ppermute | solution.py:144
  145.7 5.7 %collective-permute-start.39 = (f32[2,2,48,256]{3,2,1,0:T(8,128)S(1)}, f32[2,2,48,256]{3,2,1,0:T(8,128)S(1)}, u32[]{:S(2)}, u32[]{:S(2)}) collective-permute-start(f32[2,2,48,256]{3,2,1,0:T(8,128)S(1)} %get-tuple-element.123.refs_4_), channel_id=1, source_target_pairs={{0,1},{1,0},{2,3},{3,2},{4,5},{5,4},{6,7},{7,6},{8,9},{9,8},{10,11... | collective-permute-start | bytes 589832 | tf_op jit(solution)/shard_map/ppermute | solution.py:144
  145.8 7.1 %collective-permute-start.38 = (f32[2,2,48,256]{3,2,1,0:T(8,128)S(1)}, f32[2,2,48,256]{3,2,1,0:T(8,128)S(1)}, u32[]{:S(2)}, u32[]{:S(2)}) collective-permute-start(f32[2,2,48,256]{3,2,1,0:T(8,128)S(1)} %get-tuple-element.122.refs_4_), channel_id=1, source_target_pairs={{0,1},{1,0},{2,3},{3,2},{4,5},{5,4},{6,7},{7,6},{8,9},{9,8},{10,11... | collective-permute-start | bytes 589832 | tf_op jit(solution)/shard_map/ppermute | solution.py:144
  146.3 15.0 %collective-permute-start.42 = (f32[2,2,48,256]{3,2,1,0:T(8,128)S(1)}, f32[2,2,48,256]{3,2,1,0:T(8,128)S(1)}, u32[]{:S(2)}, u32[]{:S(2)}) collective-permute-start(f32[2,2,48,256]{3,2,1,0:T(8,128)S(1)} %get-tuple-element.112.refs_6_), channel_id=1, source_target_pairs={{0,4},{1,5},{2,6},{3,7},{4,0},{5,1},{6,2},{7,3},{8,12},{9,13},{10,... | collective-permute-start | bytes 589832 | tf_op jit(solution)/shard_map/ppermute | solution.py:144
  146.3 19.2 %collective-permute-start.44 = (f32[2,2,48,256]{3,2,1,0:T(8,128)S(1)}, f32[2,2,48,256]{3,2,1,0:T(8,128)S(1)}, u32[]{:S(2)}, u32[]{:S(2)}) collective-permute-start(f32[2,2,48,256]{3,2,1,0:T(8,128)S(1)} %get-tuple-element.121.refs_4_), channel_id=1, source_target_pairs={{0,4},{1,5},{2,6},{3,7},{4,0},{5,1},{6,2},{7,3},{8,12},{9,13},{10,... | collective-permute-start | bytes 589832 | tf_op jit(solution)/shard_map/ppermute | solution.py:144
  149.4 5.2 %collective-permute-start.37 = (f32[2,2,32,256]{3,2,1,0:T(8,128)S(1)}, f32[2,2,32,256]{3,2,1,0:T(8,128)S(1)}, u32[]{:S(2)}, u32[]{:S(2)}) collective-permute-start(f32[2,2,32,256]{3,2,1,0:T(8,128)S(1)} %get-tuple-element.125.refs_4_), channel_id=1, source_target_pairs={{0,8},{8,0},{16,24},{24,16},{1,9},{9,1},{17,25},{25,17},{2,10},{10... | collective-permute-start | bytes 393224 | tf_op jit(solution)/shard_map/ppermute | solution.py:144
  166.3 1.6 collective-permute-start.45
  166.8 1.4 collective-permute-start.43
  166.9 8.9 %collective-permute-start.41 = (f32[2,2,32,256]{3,2,1,0:T(8,128)S(1)}, f32[2,2,32,256]{3,2,1,0:T(8,128)S(1)}, u32[]{:S(2)}, u32[]{:S(2)}) collective-permute-start(f32[2,2,32,256]{3,2,1,0:T(8,128)S(1)} %get-tuple-element.135.refs_4_), channel_id=1, source_target_pairs={{0,4},{1,5},{2,6},{3,7},{4,0},{5,1},{6,2},{7,3},{8,12},{9,13},{10,... | collective-permute-start | bytes 393224 | tf_op jit(solution)/shard_map/ppermute | solution.py:144
  176.5 1.5 collective-permute-start.46
  (1 other events, 1.9 us)
where the time goes:
time: 181 us; the launch traced here: 180 us
  waiting for transfers between devices  79.5 us (44%)
  Pallas kernels  51.1 us (28%)
  starting transfers between devices  48.2 us (27%)
    ppermute x47, waiting for transfers between devices, swap(): lax.ppermute(value, axis, [(i, i ^ mask) for i in range(lax.axis_size(axi...  79.5 us
    pallas_call x57, Pallas kernels, call(): pl.pallas_call(kernel, out_shape=outs, in_specs=specs, out_specs=out_spec...  51.1 us
    ppermute x47, starting transfers between devices, swap(): lax.ppermute(value, axis, [(i, i ^ mask) for i in range(lax.axis_size(axi...  48.2 us
  transfers between devices with their start and end apart: 47, of which 17 were waited for; matrix products, arithmetic and copies ran while one was open for 0% of the time, Pallas kernels for 23%

commit v1 on v0

--- a/solution.py
+++ b/solution.py
@@ -11,8 +11,8 @@
 
 LEVELS = 5
 BF, F32 = jnp.bfloat16, jnp.float32
-SHARES = (2, 3, 3, 3, 3, 2)
-ORDER = (((9, 0),), ((0, 0),), ((9, 1),), ((1, 0),), ((9, 2),), ((0, 1),), ((0, 3),), ((0, 2),), ((1, 1),), ((0, 4),), ((1, 2),), ((0, 5),), ((2, 0),), ((9, 3),), ((3, 0),), ((9, 4),), ((2, 1),), ((1, 3),), ((4, 0),), ((2, 2),), ((3, 1),), ((1, 4),), ((3, 2),), ((2, 3),), ((4, 1),), ((5, 0),), ((4, 2),), ((1, 5),), ((2, 4), (5, 1)), ((6, 0),), ((3, 3),), ((5, 2),), ((2, 5),), ((3, 4),), ((6, 1),), ((4, 3),), ((6, 2),), ((4, 4),), ((5, 3),), ((3, 5),), ((5, 4),), ((6, 3),), ((4, 5),), ((7, 0),), ((6, 4),), ((7, 2),), ((7, 1),), ((5, 5),), ((8, 0),), ((8, 1),), ((8, 2),), ((6, 5),), ((7, 3),), ((7, 4),), ((8, 3), (8, 4)), ((7, 5),), ((8, 5),))
+SHARES = (3, 3, 4, 3, 3)
+ORDER = (((9, 0),), ((0, 0),), ((9, 1),), ((1, 0),), ((0, 2),), ((9, 4),), ((0, 1),), ((9, 3),), ((1, 2),), ((9, 2),), ((2, 0),), ((0, 3),), ((1, 1),), ((3, 0),), ((2, 2),), ((0, 4),), ((10, 1),), ((4, 0),), ((1, 3),), ((3, 2),), ((2, 1),), ((1, 4),), ((5, 0),), ((4, 2),), ((2, 3),), ((3, 1),), ((10, 0),), ((6, 0),), ((5, 2),), ((3, 3),), ((2, 4),), ((4, 1),), ((6, 2),), ((4, 3),), ((5, 1),), ((3, 4),), ((5, 3),), ((6, 1),), ((7, 0),), ((4, 4),), ((6, 3),), ((5, 4),), ((8, 0),), ((7, 1),), ((7, 2),), ((8, 1),), ((6, 4),), ((8, 2),), ((7, 3),), ((8, 3),), ((7, 4),), ((8, 4),))
 VMEM = pl.BlockSpec(memory_space=pltpu.VMEM)
 HBM = pl.BlockSpec(memory_space=pltpu.HBM)
 ANY = pl.BlockSpec(memory_space=pl.ANY)
@@ -23,8 +23,8 @@
     return high, (x - high.astype(F32)).astype(BF)
 
 
-def dot(a, b, transposed):
-    return lax.dot_general(a, b, (((1,), (1 if transposed else 0,)), ((), ())), preferred_element_type=F32)
+def dot(a, b):
+    return lax.dot_general(a, b, (((1,), (0,)), ((), ())), preferred_element_type=F32)
 
 
 def product(ur, ui, high, low, adjoint):
@@ -35,7 +35,7 @@
     tops = jnp.concatenate([rh, ih], 0)
 
     def real(k):
-        a, c = dot(both, high[k], adjoint), dot(tops, low[k], adjoint)
+        a, c = dot(both, high[k]), dot(tops, low[k])
         return a[:rows] + a[rows : 2 * rows] + c[:rows], a[2 * rows : 3 * rows] + a[3 * rows :] + c[rows:]
 
     rr, ir = real(0)
@@ -43,8 +43,15 @@
     return (rr + ii, ir - ri) if adjoint else (rr - ii, ri + ir)
 
 
-def prepare_kernel(level, own, partner, *refs):
-    high, low, buffer, sems = refs[-4:]
+def store_transposes(s, b, high, low, flipped):
+    for k in range(high.shape[2]):
+        flipped[0][s, b, k] = high[s, b, k].T
+        flipped[1][s, b, k] = low[s, b, k].T
+
+
+def prepare_kernel(level, count, own, partner, *refs):
+    high, low, *flipped = refs[-2 - count : -2]
+    buffer, sems = refs[-2:]
     boxes = high.shape[1]
     copies = [
         [pltpu.make_async_copy(source.at[level, b], buffer.at[s, b], sems.at[s, b]) for b in range(boxes)]
@@ -57,6 +64,14 @@
         for b, copy in enumerate(row):
             copy.wait()
             high[s, b], low[s, b] = split(buffer[s, b])
+            if flipped:
+                store_transposes(s, b, high, low, flipped)
+
+
+def flip_kernel(high, low, token, *flipped):
+    for s in range(high.shape[0]):
+        for b in range(high.shape[1]):
+            store_transposes(s, b, high, low, flipped)
 
 
 class Task(NamedTuple):
@@ -65,6 +80,7 @@
     ours: tuple
     theirs: tuple
     weights: int
+    flipped: int = -1
     sent: tuple = ()
     kept: int = -1
     observed: int = -1
@@ -101,6 +117,7 @@
             if task.stage < LEVELS - 1:
                 continue
             grads = [(buffer[b, 0], buffer[b, 1]) for b in boxes]
+            high, low = refs[task.flipped], refs[task.flipped + 1]
         else:
             grads = [
                 (ours[b, 0, start] + theirs[b, 0, other], ours[b, 1, start] + theirs[b, 1, other]) for b in boxes
@@ -149,7 +166,8 @@
     model, observed = (pltpu.with_memory_space_constraint(x, pltpu.VMEM) for x in (model, observed))
     stored = [pltpu.with_memory_space_constraint(x, pltpu.HBM) for x in (own_weights, partner_weights)]
     matrices = (2,) + own_weights.shape[1:]
-    weights = {}
+    weights, flipped = {}, {}
+    later = {c for group in ORDER for stage, c in group if stage == 10}
     ours = {c: (model, edges[c]) for c in range(len(SHARES))}
     theirs = dict(ours)
     results = {}
@@ -159,15 +177,23 @@
         stage, c = group[0]
         if stage == 9:
             tokens = [] if token is None else [token]
-            weights[c] = call(
-                functools.partial(prepare_kernel, c),
+            count = 2 if c in later else 4
+            made = call(
+                functools.partial(prepare_kernel, c, count),
                 stored + tokens,
                 [HBM, HBM] + [ANY] * len(tokens),
-                (pltpu.VMEM(matrices, BF),) * 2,
-                (VMEM, VMEM),
+                (pltpu.VMEM(matrices, BF),) * count,
+                (VMEM,) * count,
                 [pltpu.VMEM(matrices, F32), pltpu.SemaphoreType.DMA((2, boxes))],
             )
-            token = weights[c][0]
+            weights[c], flipped[c] = made[:2], made[2:]
+            token = made[0]
+            continue
+        if stage == 10:
+            flipped[c] = call(
+                flip_kernel, [*weights[c], token], [VMEM, VMEM, ANY], (pltpu.VMEM(matrices, BF),) * 2, (VMEM,) * 2
+            )
+            token = flipped[c][0]
             continue
         operands, specs, outs, out_specs, scratch, aliases, plans = [], [], [], [], [], {}, []
 
@@ -178,6 +204,11 @@
             operands.append(array)
             specs.append(spec)
             return len(operands) - 1
+
+        def pair_of(matrices):
+            at = operand(matrices[0])
+            operand(matrices[1])
+            return at
 
         counts = [edges[c + 1] - edges[c] for _, c in group]
         sends = exchange_of(stage)
@@ -196,10 +227,9 @@
                 "ours": (operand(ours[c][0]), ours[c][1]),
                 "theirs": (operand(theirs[c][0]), theirs[c][1]),
             }
-            pair = [x for x in weights[level]]
-            plan["weights"] = next((at for at, known in enumerate(operands) if known is pair[0]), len(operands))
-            for x in pair:
-                operand(x)
+            plan["weights"] = pair_of((weights if stage < LEVELS else flipped)[level])
+            if stage == LEVELS - 1:
+                plan["flipped"] = pair_of(flipped[level])
             if sends:
                 plan["sent"] = (0, row)
             if LEVELS - 1 <= stage < 8:

time: 181 us -> 142 us (0.78)
  waiting for transfers between devices: 79.5 us -> 48.1 us
  Pallas kernels: 51.1 us -> 42.2 us
    ppermute x47 -> x40, waiting for transfers between devices: 79.5 us -> 48.1 us  [swap(): lax.ppermute(value, axis, [(i, i ^ mask) for i in range(lax.axis_size(axi...]
    pallas_call x57 -> x52, Pallas kernels: 51.1 us -> 42.2 us  [call(): pl.pallas_call(kernel, out_shape=outs, in_specs=specs, out_specs=out_spec...]
    ppermute x47 -> x40, starting transfers between devices: 48.2 us -> 50 us  [swap(): lax.ppermute(value, axis, [(i, i ^ mask) for i in range(lax.axis_size(axi...]
  transfers between devices with their start and end apart: 47 -> 40, of which waited for: 17 -> 15; matrix products, arithmetic and copies ran while one was open for 0% -> 0% of each run, Pallas kernels for 23% -> 24%
where the time goes in v1:
time: 142 us
  starting transfers between devices  50 us (35%)
  waiting for transfers between devices  48.1 us (34%)
  Pallas kernels  42.2 us (30%)
    ppermute x40, starting transfers between devices, swap(): lax.ppermute(value, axis, [(i, i ^ mask) for i in range(lax.axis_size(axi...  50 us
    ppermute x40, waiting for transfers between devices, swap(): lax.ppermute(value, axis, [(i, i ^ mask) for i in range(lax.axis_size(axi...  48.1 us
    pallas_call x52, Pallas kernels, call(): pl.pallas_call(kernel, out_shape=outs, in_specs=specs, out_specs=out_spec...  42.2 us
  transfers between devices with their start and end apart: 40, of which 15 were waited for; matrix products, arithmetic and copies ran while one was open for 0% of the time, Pallas kernels for 24%

profile of v1, /device:TPU:1, one launch (start us, length us, event | category | flops | bytes accessed | tf_op | source)
XLA Modules:
  0.0 141.8 jit_solution(3271493574024789932)
XLA Ops:
  0.6 1.7 %shard_map.59 = (bf16[2,2,2,256,256]{4,3,2,1,0:T(8,128)(2,1)S(1)}, bf16[2,2,2,256,256]{4,3,2,1,0:T(8,128)(2,1)S(1)}) custom-call(f32[5,2,2,256,256]{4,3,2,1,0:T(8,128)} %own.9, f32[5,2,2,256,256]{4,3,2,1,0:T(8,128)} %partner.9), custom_call_target="tpu_custom_call" | custom-call | tf_op jit(solution)/shard_map/pallas_call | solution.py:142
  3.1 1.6 %shard_map.61 = (bf16[2,2,2,256,256]{4,3,2,1,0:T(8,128)(2,1)S(1)}, bf16[2,2,2,256,256]{4,3,2,1,0:T(8,128)(2,1)S(1)}) custom-call(f32[5,2,2,256,256]{4,3,2,1,0:T(8,128)} %own.9, f32[5,2,2,256,256]{4,3,2,1,0:T(8,128)} %partner.9, f32[2,2,48,256]{3,2,1,0:T(8,128)S(1)} %shard_map.60.refs_0_), custom_call_target="tpu_custom_call" | custom-call | tf_op jit(solution)/shard_map/pallas_call | solution.py:142
  6.4 3.4 %collective-permute-start.3 = (f32[2,2,48,256]{3,2,1,0:T(8,128)S(1)}, f32[2,2,48,256]{3,2,1,0:T(8,128)S(1)}, u32[]{:S(2)}, u32[]{:S(2)}) collective-permute-start(f32[2,2,48,256]{3,2,1,0:T(8,128)S(1)} %shard_map.62.refs_3_.refs_0_), channel_id=1, source_target_pairs={{0,4},{1,5},{2,6},{3,7},{4,0},{5,1},{6,2},{7,3},{8,12},{9,13},{10,... | collective-permute-start | bytes 589832 | tf_op jit(solution)/shard_map/ppermute | solution.py:161
  9.8 1.9 %shard_map.64 = (bf16[2,2,2,256,256]{4,3,2,1,0:T(8,128)(2,1)S(1)}, bf16[2,2,2,256,256]{4,3,2,1,0:T(8,128)(2,1)S(1)}, bf16[2,2,2,256,256]{4,3,2,1,0:T(8,128)(2,1)S(1)}, bf16[2,2,2,256,256]{4,3,2,1,0:T(8,128)(2,1)S(1)}) custom-call(f32[5,2,2,256,256]{4,3,2,1,0:T(8,128)} %own.9, f32[5,2,2,256,256]{4,3,2,1,0:T(8,128)} %partner.9, ...), custom_call_target="tpu_custom_call" | custom-call | tf_op jit(solution)/shard_map/pallas_call | solution.py:142
  12.3 1.9 %shard_map.66 = (bf16[2,2,2,256,256]{4,3,2,1,0:T(8,128)(2,1)S(1)}, bf16[2,2,2,256,256]{4,3,2,1,0:T(8,128)(2,1)S(1)}, bf16[2,2,2,256,256]{4,3,2,1,0:T(8,128)(2,1)S(1)}, bf16[2,2,2,256,256]{4,3,2,1,0:T(8,128)(2,1)S(1)}) custom-call(f32[5,2,2,256,256]{4,3,2,1,0:T(8,128)} %own.9, f32[5,2,2,256,256]{4,3,2,1,0:T(8,128)} %partner.9, ...), custom_call_target="tpu_custom_call" | custom-call | tf_op jit(solution)/shard_map/pallas_call | solution.py:142
  14.9 0.8 collective-permute-start.5
  15.7 1.9 %shard_map.68 = (bf16[2,2,2,256,256]{4,3,2,1,0:T(8,128)(2,1)S(1)}, bf16[2,2,2,256,256]{4,3,2,1,0:T(8,128)(2,1)S(1)}, bf16[2,2,2,256,256]{4,3,2,1,0:T(8,128)(2,1)S(1)}, bf16[2,2,2,256,256]{4,3,2,1,0:T(8,128)(2,1)S(1)}) custom-call(f32[5,2,2,256,256]{4,3,2,1,0:T(8,128)} %own.9, f32[5,2,2,256,256]{4,3,2,1,0:T(8,128)} %partner.9, ...), custom_call_target="tpu_custom_call" | custom-call | tf_op jit(solution)/shard_map/pallas_call | solution.py:142
  17.6 1.3 collective-permute-done.3.refs_1_
  19.4 1.0 collective-permute-start.4
  21.6 2.7 %collective-permute-done.4.refs_1_ = f32[2,2,48,256]{3,2,1,0:T(8,128)S(1)} collective-permute-done((f32[2,2,48,256]{3,2,1,0:T(8,128)S(1)}, f32[2,2,48,256]{3,2,1,0:T(8,128)S(1)}, u32[]{:S(2)}, u32[]{:S(2)}) %collective-permute-start.4) | collective-permute-done | bytes 196640 | tf_op jit(solution)/shard_map/ppermute | solution.py:161
  24.8 5.3 %collective-permute-done.2.refs_1_ = f32[2,2,64,256]{3,2,1,0:T(8,128)S(1)} collective-permute-done((f32[2,2,64,256]{3,2,1,0:T(8,128)S(1)}, f32[2,2,64,256]{3,2,1,0:T(8,128)S(1)}, u32[]{:S(2)}, u32[]{:S(2)}) %collective-permute-start.2) | collective-permute-done | bytes 262176 | tf_op jit(solution)/shard_map/ppermute | solution.py:161
  30.7 1.0 collective-permute-start.8
  31.7 1.2 collective-permute-start.10
  33.0 3.9 %collective-permute-start.9 = (f32[2,2,48,256]{3,2,1,0:T(8,128)S(1)}, f32[2,2,48,256]{3,2,1,0:T(8,128)S(1)}, u32[]{:S(2)}, u32[]{:S(2)}) collective-permute-start(f32[2,2,48,256]{3,2,1,0:T(8,128)S(1)} %shard_map.70.refs_4_.refs_0_), channel_id=1, source_target_pairs={{0,1},{1,0},{2,3},{3,2},{4,5},{5,4},{6,7},{7,6},{8,9},{9,8},{10,11... | collective-permute-start | bytes 589832 | tf_op jit(solution)/shard_map/ppermute | solution.py:161
  38.1 1.2 shard_map.76
  40.8 4.3 %collective-permute-start.6 = (f32[2,2,48,256]{3,2,1,0:T(8,128)S(1)}, f32[2,2,48,256]{3,2,1,0:T(8,128)S(1)}, u32[]{:S(2)}, u32[]{:S(2)}) collective-permute-start(f32[2,2,48,256]{3,2,1,0:T(8,128)S(1)} %shard_map.74.token.refs_0_), channel_id=1, source_target_pairs={{0,1},{1,0},{2,3},{3,2},{4,5},{5,4},{6,7},{7,6},{8,9},{9,8},{10,11... | collective-permute-start | bytes 589832 | tf_op jit(solution)/shard_map/ppermute | solution.py:161
  45.3 2.6 %collective-permute-start.12 = (f32[2,2,48,256]{3,2,1,0:T(8,128)S(1)}, f32[2,2,48,256]{3,2,1,0:T(8,128)S(1)}, u32[]{:S(2)}, u32[]{:S(2)}) collective-permute-start(f32[2,2,48,256]{3,2,1,0:T(8,128)S(1)} %shard_map.77.refs_4_.refs_0_), channel_id=1, source_target_pairs={{0,4},{1,5},{2,6},{3,7},{4,0},{5,1},{6,2},{7,3},{8,12},{9,13},{10,... | collective-permute-start | bytes 589832 | tf_op jit(solution)/shard_map/ppermute | solution.py:161
  49.1 2.9 %collective-permute-done.14.refs_1_ = f32[2,2,48,256]{3,2,1,0:T(8,128)S(1)} collective-permute-done((f32[2,2,48,256]{3,2,1,0:T(8,128)S(1)}, f32[2,2,48,256]{3,2,1,0:T(8,128)S(1)}, u32[]{:S(2)}, u32[]{:S(2)}) %collective-permute-start.14) | collective-permute-done | bytes 196640 | tf_op jit(solution)/shard_map/ppermute | solution.py:161
  52.5 1.3 shard_map.82
  54.9 4.8 %collective-permute-done.12.refs_1_ = f32[2,2,48,256]{3,2,1,0:T(8,128)S(1)} collective-permute-done((f32[2,2,48,256]{3,2,1,0:T(8,128)S(1)}, f32[2,2,48,256]{3,2,1,0:T(8,128)S(1)}, u32[]{:S(2)}, u32[]{:S(2)}) %collective-permute-start.12) | collective-permute-done | bytes 196640 | tf_op jit(solution)/shard_map/ppermute | solution.py:161
  61.0 1.3 collective-permute-start.20
  64.0 1.3 collective-permute-start.23
  65.3 1.2 collective-permute-done.15.refs_1_
  67.0 1.9 %collective-permute-start.22 = (f32[2,2,48,256]{3,2,1,0:T(8,128)S(1)}, f32[2,2,48,256]{3,2,1,0:T(8,128)S(1)}, u32[]{:S(2)}, u32[]{:S(2)}) collective-permute-start(f32[2,2,48,256]{3,2,1,0:T(8,128)S(1)} %shard_map.88.refs_4_.refs_0_), channel_id=1, source_target_pairs={{0,16},{8,24},{16,0},{24,8},{1,17},{9,25},{17,1},{25,9},{2,18},{10... | collective-permute-start | bytes 589832 | tf_op jit(solution)/shard_map/ppermute | solution.py:161
  69.4 1.2 shard_map.90
  71.1 1.2 collective-permute-start.19
  73.0 1.2 shard_map.92
  74.2 2.1 %collective-permute-start.27 = (f32[2,2,48,256]{3,2,1,0:T(8,128)S(1)}, f32[2,2,48,256]{3,2,1,0:T(8,128)S(1)}, u32[]{:S(2)}, u32[]{:S(2)}) collective-permute-start(f32[2,2,48,256]{3,2,1,0:T(8,128)S(1)} %get-tuple-element.109.refs_4_), channel_id=1, source_target_pairs={{0,16},{8,24},{16,0},{24,8},{1,17},{9,25},{17,1},{25,9},{2,18},{10... | collective-permute-start | bytes 589832 | tf_op jit(solution)/shard_map/ppermute | solution.py:161
  77.5 1.9 %collective-permute-start.25 = (f32[2,2,48,256]{3,2,1,0:T(8,128)S(1)}, f32[2,2,48,256]{3,2,1,0:T(8,128)S(1)}, u32[]{:S(2)}, u32[]{:S(2)}) collective-permute-start(f32[2,2,48,256]{3,2,1,0:T(8,128)S(1)} %get-tuple-element.101.refs_4_), channel_id=1, source_target_pairs={{0,4},{1,5},{2,6},{3,7},{4,0},{5,1},{6,2},{7,3},{8,12},{9,13},{10,... | collective-permute-start | bytes 589832 | tf_op jit(solution)/shard_map/ppermute | solution.py:161
  79.9 1.2 collective-permute-start.24
  82.1 1.5 %collective-permute-start.29 = (f32[2,2,48,256]{3,2,1,0:T(8,128)S(1)}, f32[2,2,48,256]{3,2,1,0:T(8,128)S(1)}, u32[]{:S(2)}, u32[]{:S(2)}) collective-permute-start(f32[2,2,48,256]{3,2,1,0:T(8,128)S(1)} %get-tuple-element.116.refs_4_), channel_id=1, source_target_pairs={{0,8},{8,0},{16,24},{24,16},{1,9},{9,1},{17,25},{25,17},{2,10},{10... | collective-permute-start | bytes 589832 | tf_op jit(solution)/shard_map/ppermute | solution.py:161
  84.7 1.3 collective-permute-done.24.refs_1_
  85.9 1.2 shard_map.98
  87.2 1.3 collective-permute-start.28
  88.5 10.9 %collective-permute-start.32 = (f32[2,2,48,256]{3,2,1,0:T(8,128)S(1)}, f32[2,2,48,256]{3,2,1,0:T(8,128)S(1)}, u32[]{:S(2)}, u32[]{:S(2)}) collective-permute-start(f32[2,2,48,256]{3,2,1,0:T(8,128)S(1)} %get-tuple-element.118.refs_8_), channel_id=1, source_target_pairs={{0,1},{1,0},{2,3},{3,2},{4,5},{5,4},{6,7},{7,6},{8,9},{9,8},{10,11... | collective-permute-start | bytes 589832 | tf_op jit(solution)/shard_map/ppermute | solution.py:161
  100.5 1.2 shard_map.101
  101.7 9.2 %collective-permute-done.31.refs_1_ = f32[2,2,48,256]{3,2,1,0:T(8,128)S(1)} collective-permute-done((f32[2,2,48,256]{3,2,1,0:T(8,128)S(1)}, f32[2,2,48,256]{3,2,1,0:T(8,128)S(1)}, u32[]{:S(2)}, u32[]{:S(2)}) %collective-permute-start.31) | collective-permute-done | bytes 196640 | tf_op jit(solution)/shard_map/ppermute | solution.py:161
  112.1 0.9 collective-permute-start.37
  113.1 1.1 collective-permute-start.30
  114.4 1.2 shard_map.104
  115.7 3.4 %collective-permute-done.30.refs_1_ = f32[2,2,48,256]{3,2,1,0:T(8,128)S(1)} collective-permute-done((f32[2,2,48,256]{3,2,1,0:T(8,128)S(1)}, f32[2,2,48,256]{3,2,1,0:T(8,128)S(1)}, u32[]{:S(2)}, u32[]{:S(2)}) %collective-permute-start.30) | collective-permute-done | bytes 196640 | tf_op jit(solution)/shard_map/ppermute | solution.py:161
  119.6 1.3 shard_map.106
  120.9 3.7 %collective-permute-done.36.refs_1_ = f32[2,2,48,256]{3,2,1,0:T(8,128)S(1)} collective-permute-done((f32[2,2,48,256]{3,2,1,0:T(8,128)S(1)}, f32[2,2,48,256]{3,2,1,0:T(8,128)S(1)}, u32[]{:S(2)}, u32[]{:S(2)}) %collective-permute-start.36) | collective-permute-done | bytes 196640 | tf_op jit(solution)/shard_map/ppermute | solution.py:161
  125.7 1.1 collective-permute-done.38.refs_1_
  126.8 1.2 shard_map.108
  128.0 9.7 %collective-permute-done.35.refs_1_ = f32[2,2,48,256]{3,2,1,0:T(8,128)S(1)} collective-permute-done((f32[2,2,48,256]{3,2,1,0:T(8,128)S(1)}, f32[2,2,48,256]{3,2,1,0:T(8,128)S(1)}, u32[]{:S(2)}, u32[]{:S(2)}) %collective-permute-start.35) | collective-permute-done | bytes 196640 | tf_op jit(solution)/shard_map/ppermute | solution.py:161
  138.8 1.1 collective-permute-done.39.refs_1_
  139.8 1.8 %shard_map.110 = (f32[8,128]{1,0:T(8,128)}, f32[2,2,256,256]{3,2,1,0:T(8,128)}) custom-call(f32[2,2,48,256]{3,2,1,0:T(8,128)S(1)} %get-tuple-element.146.refs_0_, f32[2,2,48,256]{3,2,1,0:T(8,128)S(1)} %collective-permute-done.39.refs_1_, bf16[2,2,2,256,256]{4,3,2,1,0:T(8,128)(2,1)S(1)} %get-tuple-element.100.refs_4_.refs_2_, ...), custom_call_target="tpu_custom_call", output_to_operand_aliasing={{1}: (4, {})} | custom-call | tf_op jit(solution)/shard_map/pallas_call | solution.py:142
  (88 shorter events, 25.8 us)
Async XLA Ops:
  0.6 1.9 %copy-start = (f32[2,2,256,256]{3,2,1,0:T(8,128)S(1)}, f32[2,2,256,256]{3,2,1,0:T(8,128)}, u32[]{:S(2)}) copy-start(f32[2,2,256,256]{3,2,1,0:T(8,128)} %refs_0_.9) | copy-start | bytes 3145732
  3.0 1.7 %collective-permute-start = (f32[2,2,48,256]{3,2,1,0:T(8,128)S(1)}, f32[2,2,48,256]{3,2,1,0:T(8,128)S(1)}, u32[]{:S(2)}, u32[]{:S(2)}) collective-permute-start(f32[2,2,48,256]{3,2,1,0:T(8,128)S(1)} %shard_map.60.refs_0_), channel_id=1, source_target_pairs={{0,1},{1,0},{2,3},{3,2},{4,5},{5,4},{6,7},{7,6},{8,9},{9,8},{10,11... | collective-permute-start | bytes 589832 | tf_op jit(solution)/shard_map/ppermute | solution.py:161
  5.9 8.3 %collective-permute-start.1 = (f32[2,2,64,256]{3,2,1,0:T(8,128)S(1)}, f32[2,2,64,256]{3,2,1,0:T(8,128)S(1)}, u32[]{:S(2)}, u32[]{:S(2)}) collective-permute-start(f32[2,2,64,256]{3,2,1,0:T(8,128)S(1)} %shard_map.63.refs_0_), channel_id=1, source_target_pairs={{0,1},{1,0},{2,3},{3,2},{4,5},{5,4},{6,7},{7,6},{8,9},{9,8},{10,11... | collective-permute-start | bytes 786440 | tf_op jit(solution)/shard_map/ppermute | solution.py:161
  6.4 12.4 %collective-permute-start.3 = (f32[2,2,48,256]{3,2,1,0:T(8,128)S(1)}, f32[2,2,48,256]{3,2,1,0:T(8,128)S(1)}, u32[]{:S(2)}, u32[]{:S(2)}) collective-permute-start(f32[2,2,48,256]{3,2,1,0:T(8,128)S(1)} %shard_map.62.refs_3_.refs_0_), channel_id=1, source_target_pairs={{0,4},{1,5},{2,6},{3,7},{4,0},{5,1},{6,2},{7,3},{8,12},{9,13},{10,... | collective-permute-start | bytes 589832 | tf_op jit(solution)/shard_map/ppermute | solution.py:161
  14.8 15.3 %collective-permute-start.2 = (f32[2,2,64,256]{3,2,1,0:T(8,128)S(1)}, f32[2,2,64,256]{3,2,1,0:T(8,128)S(1)}, u32[]{:S(2)}, u32[]{:S(2)}) collective-permute-start(f32[2,2,64,256]{3,2,1,0:T(8,128)S(1)} %shard_map.67.refs_0_), channel_id=1, source_target_pairs={{0,4},{1,5},{2,6},{3,7},{4,0},{5,1},{6,2},{7,3},{8,12},{9,13},{10,... | collective-permute-start | bytes 786440 | tf_op jit(solution)/shard_map/ppermute | solution.py:161
  14.9 6.1 %collective-permute-start.5 = (f32[2,2,48,256]{3,2,1,0:T(8,128)S(1)}, f32[2,2,48,256]{3,2,1,0:T(8,128)S(1)}, u32[]{:S(2)}, u32[]{:S(2)}) collective-permute-start(f32[2,2,48,256]{3,2,1,0:T(8,128)S(1)} %shard_map.65.refs_0_), channel_id=1, source_target_pairs={{0,1},{1,0},{2,3},{3,2},{4,5},{5,4},{6,7},{7,6},{8,9},{9,8},{10,11... | collective-permute-start | bytes 589832 | tf_op jit(solution)/shard_map/ppermute | solution.py:161
  19.4 4.9 %collective-permute-start.4 = (f32[2,2,48,256]{3,2,1,0:T(8,128)S(1)}, f32[2,2,48,256]{3,2,1,0:T(8,128)S(1)}, u32[]{:S(2)}, u32[]{:S(2)}) collective-permute-start(f32[2,2,48,256]{3,2,1,0:T(8,128)S(1)} %shard_map.69.refs_3_.refs_0_), channel_id=1, source_target_pairs={{0,8},{8,0},{16,24},{24,16},{1,9},{9,1},{17,25},{25,17},{2,10},{10... | collective-permute-start | bytes 589832 | tf_op jit(solution)/shard_map/ppermute | solution.py:161
  24.3 13.8 %copy-start.1 = (f32[2,2,256,256]{3,2,1,0:T(8,128)S(1)}, f32[2,2,256,256]{3,2,1,0:T(8,128)}, u32[]{:S(2)}) copy-start(f32[2,2,256,256]{3,2,1,0:T(8,128)} %refs_6_.9) | copy-start | bytes 3145732
  30.7 9.2 %collective-permute-start.8 = (f32[2,2,64,256]{3,2,1,0:T(8,128)S(1)}, f32[2,2,64,256]{3,2,1,0:T(8,128)S(1)}, u32[]{:S(2)}, u32[]{:S(2)}) collective-permute-start(f32[2,2,64,256]{3,2,1,0:T(8,128)S(1)} %shard_map.73.refs_3_.refs_0_), channel_id=1, source_target_pairs={{0,8},{8,0},{16,24},{24,16},{1,9},{9,1},{17,25},{25,17},{2,10},{10... | collective-permute-start | bytes 786440 | tf_op jit(solution)/shard_map/ppermute | solution.py:161
  31.7 6.3 %collective-permute-start.10 = (f32[2,2,48,256]{3,2,1,0:T(8,128)S(1)}, f32[2,2,48,256]{3,2,1,0:T(8,128)S(1)}, u32[]{:S(2)}, u32[]{:S(2)}) collective-permute-start(f32[2,2,48,256]{3,2,1,0:T(8,128)S(1)} %shard_map.72.refs_4_.refs_0_), channel_id=1, source_target_pairs={{0,16},{8,24},{16,0},{24,8},{1,17},{9,25},{17,1},{25,9},{2,18},{10... | collective-permute-start | bytes 589832 | tf_op jit(solution)/shard_map/ppermute | solution.py:161
  33.0 6.4 %collective-permute-start.9 = (f32[2,2,48,256]{3,2,1,0:T(8,128)S(1)}, f32[2,2,48,256]{3,2,1,0:T(8,128)S(1)}, u32[]{:S(2)}, u32[]{:S(2)}) collective-permute-start(f32[2,2,48,256]{3,2,1,0:T(8,128)S(1)} %shard_map.70.refs_4_.refs_0_), channel_id=1, source_target_pairs={{0,1},{1,0},{2,3},{3,2},{4,5},{5,4},{6,7},{7,6},{8,9},{9,8},{10,11... | collective-permute-start | bytes 589832 | tf_op jit(solution)/shard_map/ppermute | solution.py:161
  40.5 12.0 %collective-permute-start.13 = (f32[2,2,64,256]{3,2,1,0:T(8,128)S(1)}, f32[2,2,64,256]{3,2,1,0:T(8,128)S(1)}, u32[]{:S(2)}, u32[]{:S(2)}) collective-permute-start(f32[2,2,64,256]{3,2,1,0:T(8,128)S(1)} %shard_map.78.refs_4_.refs_0_), channel_id=1, source_target_pairs={{0,16},{8,24},{16,0},{24,8},{1,17},{9,25},{17,1},{25,9},{2,18},{10... | collective-permute-start | bytes 786440 | tf_op jit(solution)/shard_map/ppermute | solution.py:161
  40.8 7.2 %collective-permute-start.7 = (f32[2,2,48,256]{3,2,1,0:T(8,128)S(1)}, f32[2,2,48,256]{3,2,1,0:T(8,128)S(1)}, u32[]{:S(2)}, u32[]{:S(2)}) collective-permute-start(f32[2,2,48,256]{3,2,1,0:T(8,128)S(1)} %shard_map.71.refs_4_.refs_0_), channel_id=1, source_target_pairs={{0,4},{1,5},{2,6},{3,7},{4,0},{5,1},{6,2},{7,3},{8,12},{9,13},{10,... | collective-permute-start | bytes 589832 | tf_op jit(solution)/shard_map/ppermute | solution.py:161
  40.8 7.8 %collective-permute-start.6 = (f32[2,2,48,256]{3,2,1,0:T(8,128)S(1)}, f32[2,2,48,256]{3,2,1,0:T(8,128)S(1)}, u32[]{:S(2)}, u32[]{:S(2)}) collective-permute-start(f32[2,2,48,256]{3,2,1,0:T(8,128)S(1)} %shard_map.74.token.refs_0_), channel_id=1, source_target_pairs={{0,1},{1,0},{2,3},{3,2},{4,5},{5,4},{6,7},{7,6},{8,9},{9,8},{10,11... | collective-permute-start | bytes 589832 | tf_op jit(solution)/shard_map/ppermute | solution.py:161
  45.1 6.9 %collective-permute-start.14 = (f32[2,2,48,256]{3,2,1,0:T(8,128)S(1)}, f32[2,2,48,256]{3,2,1,0:T(8,128)S(1)}, u32[]{:S(2)}, u32[]{:S(2)}) collective-permute-start(f32[2,2,48,256]{3,2,1,0:T(8,128)S(1)} %get-tuple-element.89.refs_4_), channel_id=1, source_target_pairs={{0,16},{8,24},{16,0},{24,8},{1,17},{9,25},{17,1},{25,9},{2,18},{10... | collective-permute-start | bytes 589832 | tf_op jit(solution)/shard_map/ppermute | solution.py:161
  45.3 14.4 %collective-permute-start.12 = (f32[2,2,48,256]{3,2,1,0:T(8,128)S(1)}, f32[2,2,48,256]{3,2,1,0:T(8,128)S(1)}, u32[]{:S(2)}, u32[]{:S(2)}) collective-permute-start(f32[2,2,48,256]{3,2,1,0:T(8,128)S(1)} %shard_map.77.refs_4_.refs_0_), channel_id=1, source_target_pairs={{0,4},{1,5},{2,6},{3,7},{4,0},{5,1},{6,2},{7,3},{8,12},{9,13},{10,... | collective-permute-start | bytes 589832 | tf_op jit(solution)/shard_map/ppermute | solution.py:161
  48.5 11.9 %collective-permute-start.18 = (f32[2,2,48,256]{3,2,1,0:T(8,128)S(1)}, f32[2,2,48,256]{3,2,1,0:T(8,128)S(1)}, u32[]{:S(2)}, u32[]{:S(2)}) collective-permute-start(f32[2,2,48,256]{3,2,1,0:T(8,128)S(1)} %shard_map.79.refs_4_.refs_0_), channel_id=1, source_target_pairs={{0,8},{8,0},{16,24},{24,16},{1,9},{9,1},{17,25},{25,17},{2,10},{10... | collective-permute-start | bytes 589832 | tf_op jit(solution)/shard_map/ppermute | solution.py:161
  53.9 9.6 %collective-permute-start.16 = (f32[2,2,64,256]{3,2,1,0:T(8,128)S(1)}, f32[2,2,64,256]{3,2,1,0:T(8,128)S(1)}, u32[]{:S(2)}, u32[]{:S(2)}) collective-permute-start(f32[2,2,64,256]{3,2,1,0:T(8,128)S(1)} %get-tuple-element.95.refs_4_), channel_id=1, source_target_pairs={{0,16},{8,24},{16,0},{24,8},{1,17},{9,25},{17,1},{25,9},{2,18},{10... | collective-permute-start | bytes 786440 | tf_op jit(solution)/shard_map/ppermute | solution.py:161
  54.2 8.7 %collective-permute-start.17 = (f32[2,2,48,256]{3,2,1,0:T(8,128)S(1)}, f32[2,2,48,256]{3,2,1,0:T(8,128)S(1)}, u32[]{:S(2)}, u32[]{:S(2)}) collective-permute-start(f32[2,2,48,256]{3,2,1,0:T(8,128)S(1)} %get-tuple-element.94.refs_8_), channel_id=1, source_target_pairs={{0,8},{8,0},{16,24},{24,16},{1,9},{9,1},{17,25},{25,17},{2,10},{10... | collective-permute-start | bytes 589832 | tf_op jit(solution)/shard_map/ppermute | solution.py:161
  60.2 6.2 %collective-permute-start.15 = (f32[2,2,48,256]{3,2,1,0:T(8,128)S(1)}, f32[2,2,48,256]{3,2,1,0:T(8,128)S(1)}, u32[]{:S(2)}, u32[]{:S(2)}) collective-permute-start(f32[2,2,48,256]{3,2,1,0:T(8,128)S(1)} %shard_map.83.refs_4_.refs_0_), channel_id=1, source_target_pairs={{0,8},{8,0},{16,24},{24,16},{1,9},{9,1},{17,25},{25,17},{2,10},{10... | collective-permute-start | bytes 589832 | tf_op jit(solution)/shard_map/ppermute | solution.py:161
  60.4 8.5 %collective-permute-start.11 = (f32[2,2,48,256]{3,2,1,0:T(8,128)S(1)}, f32[2,2,48,256]{3,2,1,0:T(8,128)S(1)}, u32[]{:S(2)}, u32[]{:S(2)}) collective-permute-start(f32[2,2,48,256]{3,2,1,0:T(8,128)S(1)} %shard_map.80.refs_4_.refs_0_), channel_id=1, source_target_pairs={{0,4},{1,5},{2,6},{3,7},{4,0},{5,1},{6,2},{7,3},{8,12},{9,13},{10,... | collective-permute-start | bytes 589832 | tf_op jit(solution)/shard_map/ppermute | solution.py:161
  61.0 8.5 %collective-permute-start.20 = (f32[2,2,48,256]{3,2,1,0:T(8,128)S(1)}, f32[2,2,48,256]{3,2,1,0:T(8,128)S(1)}, u32[]{:S(2)}, u32[]{:S(2)}) collective-permute-start(f32[2,2,48,256]{3,2,1,0:T(8,128)S(1)} %shard_map.84.token.refs_0_), channel_id=1, source_target_pairs={{0,16},{8,24},{16,0},{24,8},{1,17},{9,25},{17,1},{25,9},{2,18},{10... | collective-permute-start | bytes 589832 | tf_op jit(solution)/shard_map/ppermute | solution.py:161
  64.0 8.4 %collective-permute-start.23 = (f32[2,2,64,256]{3,2,1,0:T(8,128)S(1)}, f32[2,2,64,256]{3,2,1,0:T(8,128)S(1)}, u32[]{:S(2)}, u32[]{:S(2)}) collective-permute-start(f32[2,2,64,256]{3,2,1,0:T(8,128)S(1)} %get-tuple-element.102.refs_4_), channel_id=1, source_target_pairs={{0,8},{8,0},{16,24},{24,16},{1,9},{9,1},{17,25},{25,17},{2,10},{10... | collective-permute-start | bytes 786440 | tf_op jit(solution)/shard_map/ppermute | solution.py:161
  67.0 6.0 %collective-permute-start.22 = (f32[2,2,48,256]{3,2,1,0:T(8,128)S(1)}, f32[2,2,48,256]{3,2,1,0:T(8,128)S(1)}, u32[]{:S(2)}, u32[]{:S(2)}) collective-permute-start(f32[2,2,48,256]{3,2,1,0:T(8,128)S(1)} %shard_map.88.refs_4_.refs_0_), channel_id=1, source_target_pairs={{0,16},{8,24},{16,0},{24,8},{1,17},{9,25},{17,1},{25,9},{2,18},{10... | collective-permute-start | bytes 589832 | tf_op jit(solution)/shard_map/ppermute | solution.py:161
  70.7 5.6 %collective-permute-start.21 = (f32[2,2,48,256]{3,2,1,0:T(8,128)S(1)}, f32[2,2,48,256]{3,2,1,0:T(8,128)S(1)}, u32[]{:S(2)}, u32[]{:S(2)}) collective-permute-start(f32[2,2,48,256]{3,2,1,0:T(8,128)S(1)} %get-tuple-element.105.refs_4_), channel_id=1, source_target_pairs={{0,16},{8,24},{16,0},{24,8},{1,17},{9,25},{17,1},{25,9},{2,18},{10... | collective-permute-start | bytes 589832 | tf_op jit(solution)/shard_map/ppermute | solution.py:161
  71.1 8.2 %collective-permute-start.19 = (f32[2,2,48,256]{3,2,1,0:T(8,128)S(1)}, f32[2,2,48,256]{3,2,1,0:T(8,128)S(1)}, u32[]{:S(2)}, u32[]{:S(2)}) collective-permute-start(f32[2,2,48,256]{3,2,1,0:T(8,128)S(1)} %shard_map.89.refs_8_.refs_0_), channel_id=1, source_target_pairs={{0,8},{8,0},{16,24},{24,16},{1,9},{9,1},{17,25},{25,17},{2,10},{10... | collective-permute-start | bytes 589832 | tf_op jit(solution)/shard_map/ppermute | solution.py:161
  74.2 7.3 %collective-permute-start.27 = (f32[2,2,48,256]{3,2,1,0:T(8,128)S(1)}, f32[2,2,48,256]{3,2,1,0:T(8,128)S(1)}, u32[]{:S(2)}, u32[]{:S(2)}) collective-permute-start(f32[2,2,48,256]{3,2,1,0:T(8,128)S(1)} %get-tuple-element.109.refs_4_), channel_id=1, source_target_pairs={{0,16},{8,24},{16,0},{24,8},{1,17},{9,25},{17,1},{25,9},{2,18},{10... | collective-permute-start | bytes 589832 | tf_op jit(solution)/shard_map/ppermute | solution.py:161
  76.9 6.7 %collective-permute-start.26 = (f32[2,2,48,256]{3,2,1,0:T(8,128)S(1)}, f32[2,2,48,256]{3,2,1,0:T(8,128)S(1)}, u32[]{:S(2)}, u32[]{:S(2)}) collective-permute-start(f32[2,2,48,256]{3,2,1,0:T(8,128)S(1)} %get-tuple-element.110.refs_4_), channel_id=1, source_target_pairs={{0,8},{8,0},{16,24},{24,16},{1,9},{9,1},{17,25},{25,17},{2,10},{10... | collective-permute-start | bytes 589832 | tf_op jit(solution)/shard_map/ppermute | solution.py:161
  77.5 6.7 %collective-permute-start.25 = (f32[2,2,48,256]{3,2,1,0:T(8,128)S(1)}, f32[2,2,48,256]{3,2,1,0:T(8,128)S(1)}, u32[]{:S(2)}, u32[]{:S(2)}) collective-permute-start(f32[2,2,48,256]{3,2,1,0:T(8,128)S(1)} %get-tuple-element.101.refs_4_), channel_id=1, source_target_pairs={{0,4},{1,5},{2,6},{3,7},{4,0},{5,1},{6,2},{7,3},{8,12},{9,13},{10,... | collective-permute-start | bytes 589832 | tf_op jit(solution)/shard_map/ppermute | solution.py:161
  79.9 6.1 %collective-permute-start.24 = (f32[2,2,48,256]{3,2,1,0:T(8,128)S(1)}, f32[2,2,48,256]{3,2,1,0:T(8,128)S(1)}, u32[]{:S(2)}, u32[]{:S(2)}) collective-permute-start(f32[2,2,48,256]{3,2,1,0:T(8,128)S(1)} %shard_map.94.refs_4_.refs_0_), channel_id=1, source_target_pairs={{0,16},{8,24},{16,0},{24,8},{1,17},{9,25},{17,1},{25,9},{2,18},{10... | collective-permute-start | bytes 589832 | tf_op jit(solution)/shard_map/ppermute | solution.py:161
  81.1 30.4 %collective-permute-start.34 = (f32[2,2,64,256]{3,2,1,0:T(8,128)S(1)}, f32[2,2,64,256]{3,2,1,0:T(8,128)S(1)}, u32[]{:S(2)}, u32[]{:S(2)}) collective-permute-start(f32[2,2,64,256]{3,2,1,0:T(8,128)S(1)} %get-tuple-element.108.refs_8_), channel_id=1, source_target_pairs={{0,4},{1,5},{2,6},{3,7},{4,0},{5,1},{6,2},{7,3},{8,12},{9,13},{10,... | collective-permute-start | bytes 786440 | tf_op jit(solution)/shard_map/ppermute | solution.py:161
  82.1 17.3 %collective-permute-start.29 = (f32[2,2,48,256]{3,2,1,0:T(8,128)S(1)}, f32[2,2,48,256]{3,2,1,0:T(8,128)S(1)}, u32[]{:S(2)}, u32[]{:S(2)}) collective-permute-start(f32[2,2,48,256]{3,2,1,0:T(8,128)S(1)} %get-tuple-element.116.refs_4_), channel_id=1, source_target_pairs={{0,8},{8,0},{16,24},{24,16},{1,9},{9,1},{17,25},{25,17},{2,10},{10... | collective-permute-start | bytes 589832 | tf_op jit(solution)/shard_map/ppermute | solution.py:161
  87.2 12.7 %collective-permute-start.28 = (f32[2,2,48,256]{3,2,1,0:T(8,128)S(1)}, f32[2,2,48,256]{3,2,1,0:T(8,128)S(1)}, u32[]{:S(2)}, u32[]{:S(2)}) collective-permute-start(f32[2,2,48,256]{3,2,1,0:T(8,128)S(1)} %get-tuple-element.121.refs_4_), channel_id=1, source_target_pairs={{0,16},{8,24},{16,0},{24,8},{1,17},{9,25},{17,1},{25,9},{2,18},{10... | collective-permute-start | bytes 589832 | tf_op jit(solution)/shard_map/ppermute | solution.py:161
  88.5 12.0 %collective-permute-start.32 = (f32[2,2,48,256]{3,2,1,0:T(8,128)S(1)}, f32[2,2,48,256]{3,2,1,0:T(8,128)S(1)}, u32[]{:S(2)}, u32[]{:S(2)}) collective-permute-start(f32[2,2,48,256]{3,2,1,0:T(8,128)S(1)} %get-tuple-element.118.refs_8_), channel_id=1, source_target_pairs={{0,1},{1,0},{2,3},{3,2},{4,5},{5,4},{6,7},{7,6},{8,9},{9,8},{10,11... | collective-permute-start | bytes 589832 | tf_op jit(solution)/shard_map/ppermute | solution.py:161
  99.4 11.6 %collective-permute-start.31 = (f32[2,2,48,256]{3,2,1,0:T(8,128)S(1)}, f32[2,2,48,256]{3,2,1,0:T(8,128)S(1)}, u32[]{:S(2)}, u32[]{:S(2)}) collective-permute-start(f32[2,2,48,256]{3,2,1,0:T(8,128)S(1)} %get-tuple-element.117.refs_4_), channel_id=1, source_target_pairs={{0,4},{1,5},{2,6},{3,7},{4,0},{5,1},{6,2},{7,3},{8,12},{9,13},{10,... | collective-permute-start | bytes 589832 | tf_op jit(solution)/shard_map/ppermute | solution.py:161
  112.1 7.6 %collective-permute-start.37 = (f32[2,2,64,256]{3,2,1,0:T(8,128)S(1)}, f32[2,2,64,256]{3,2,1,0:T(8,128)S(1)}, u32[]{:S(2)}, u32[]{:S(2)}) collective-permute-start(f32[2,2,64,256]{3,2,1,0:T(8,128)S(1)} %get-tuple-element.134.refs_5_), channel_id=1, source_target_pairs={{0,1},{1,0},{2,3},{3,2},{4,5},{5,4},{6,7},{7,6},{8,9},{9,8},{10,11... | collective-permute-start | bytes 786440 | tf_op jit(solution)/shard_map/ppermute | solution.py:161
  113.0 1.4 %collective-permute-start.33 = (f32[2,2,48,256]{3,2,1,0:T(8,128)S(1)}, f32[2,2,48,256]{3,2,1,0:T(8,128)S(1)}, u32[]{:S(2)}, u32[]{:S(2)}) collective-permute-start(f32[2,2,48,256]{3,2,1,0:T(8,128)S(1)} %get-tuple-element.131.refs_4_), channel_id=1, source_target_pairs={{0,1},{1,0},{2,3},{3,2},{4,5},{5,4},{6,7},{7,6},{8,9},{9,8},{10,11... | collective-permute-start | bytes 589832 | tf_op jit(solution)/shard_map/ppermute | solution.py:161
  113.1 6.0 %collective-permute-start.30 = (f32[2,2,48,256]{3,2,1,0:T(8,128)S(1)}, f32[2,2,48,256]{3,2,1,0:T(8,128)S(1)}, u32[]{:S(2)}, u32[]{:S(2)}) collective-permute-start(f32[2,2,48,256]{3,2,1,0:T(8,128)S(1)} %get-tuple-element.125.refs_4_), channel_id=1, source_target_pairs={{0,8},{8,0},{16,24},{24,16},{1,9},{9,1},{17,25},{25,17},{2,10},{10... | collective-permute-start | bytes 589832 | tf_op jit(solution)/shard_map/ppermute | solution.py:161
  114.2 10.5 %collective-permute-start.36 = (f32[2,2,48,256]{3,2,1,0:T(8,128)S(1)}, f32[2,2,48,256]{3,2,1,0:T(8,128)S(1)}, u32[]{:S(2)}, u32[]{:S(2)}) collective-permute-start(f32[2,2,48,256]{3,2,1,0:T(8,128)S(1)} %get-tuple-element.123.refs_4_), channel_id=1, source_target_pairs={{0,4},{1,5},{2,6},{3,7},{4,0},{5,1},{6,2},{7,3},{8,12},{9,13},{10,... | collective-permute-start | bytes 589832 | tf_op jit(solution)/shard_map/ppermute | solution.py:161
  125.2 1.6 %collective-permute-start.38 = (f32[2,2,48,256]{3,2,1,0:T(8,128)S(1)}, f32[2,2,48,256]{3,2,1,0:T(8,128)S(1)}, u32[]{:S(2)}, u32[]{:S(2)}) collective-permute-start(f32[2,2,48,256]{3,2,1,0:T(8,128)S(1)} %get-tuple-element.143.refs_5_), channel_id=1, source_target_pairs={{0,1},{1,0},{2,3},{3,2},{4,5},{5,4},{6,7},{7,6},{8,9},{9,8},{10,11... | collective-permute-start | bytes 589832 | tf_op jit(solution)/shard_map/ppermute | solution.py:161
  125.7 12.0 %collective-permute-start.35 = (f32[2,2,48,256]{3,2,1,0:T(8,128)S(1)}, f32[2,2,48,256]{3,2,1,0:T(8,128)S(1)}, u32[]{:S(2)}, u32[]{:S(2)}) collective-permute-start(f32[2,2,48,256]{3,2,1,0:T(8,128)S(1)} %get-tuple-element.137.refs_5_), channel_id=1, source_target_pairs={{0,4},{1,5},{2,6},{3,7},{4,0},{5,1},{6,2},{7,3},{8,12},{9,13},{10,... | collective-permute-start | bytes 589832 | tf_op jit(solution)/shard_map/ppermute | solution.py:161
  138.3 1.6 %collective-permute-start.39 = (f32[2,2,48,256]{3,2,1,0:T(8,128)S(1)}, f32[2,2,48,256]{3,2,1,0:T(8,128)S(1)}, u32[]{:S(2)}, u32[]{:S(2)}) collective-permute-start(f32[2,2,48,256]{3,2,1,0:T(8,128)S(1)} %get-tuple-element.147.refs_5_), channel_id=1, source_target_pairs={{0,1},{1,0},{2,3},{3,2},{4,5},{5,4},{6,7},{7,6},{8,9},{9,8},{10,11... | collective-permute-start | bytes 589832 | tf_op jit(solution)/shard_map/ppermute | solution.py:161
